TPU v7x, 128 devices: a whole 4x4x4 slice. The times are simulated.
128 devices in a mesh: role: 2 (over core), seq: 16 (over z, x), tp: 4 (over y).
Axes of the slice: x: 4, y: 4, z: 4, core: 2. Of those that a mesh axis runs over, the one named last changes fastest.
Arguments:
- merger_hidden: bfloat16 [2048, 5120], P(('role', 'seq'), 'tp'), may hold values from -6 to 6
- merger_out: bfloat16 [5120, 8192], P('tp', ('role', 'seq')), may hold values from -0.078125 to 0.078125
- row_position: int32 [2048], P(('role', 'seq')), may hold values from -1 to 8191, as said below
- prompt_embeds: bfloat16 [8192, 8192], P(('role', 'seq'), 'tp'), may hold values from -300 to 300
- norm_gain: bfloat16 [8192], P('tp'), may hold values from 0.099609375 to 1.8984375
- query_weight: bfloat16 [8192, 4096], P(None, 'tp'), may hold values from -2.762136 to 2.762136
- key_weight: bfloat16 [8192, 512], P(None, 'tp'), may hold values from -0.06629126 to 0.06629126
- value_weight: bfloat16 [8192, 512], P(None, 'tp'), may hold values from -0.0625 to 0.0625
Outputs:
- stream: bfloat16 [8192, 8192], P(('role', 'seq'), 'tp')
- context: bfloat16 [8192, 4096], P(('role', 'seq'), 'tp')
Inputs may be any that keep to these rules, and one draw needn't show every extreme that they name: `row_position`: the live slots of each device's 64 come first and hold distinct prompt positions, distinct over all devices; the other slots hold -1. Of one device's slots at most 4 hold positions of one owner's block (positions j * 256 to (j + 1) * 256 - 1); every device has 4 or more live slots.
All inputs are finite; a program needn't handle non-finite values.
Results may differ from a plain program's by a relative error of at most 0.012.
The roundings to bfloat16 on the way count: a program that leaves them out, or rounds other values in their place, can miss the bound.
Values may be sent and summed in bfloat16 or wider, within the bound.
A program may use at most 192 MiB of HBM per device.

v0:
```python
import math

import jax
import jax.numpy as jnp
from jax import lax
from jax.sharding import PartitionSpec as P

HEAD_DIM = 128


def split_up(x, dim, length):
    before, after = (x.shape[:dim], x.shape[dim + 1 :])
    return jnp.moveaxis(x.reshape(*before, length, -1, *after), dim, 0)


def in_order(blocks, dim):
    lengths = list(blocks.shape[1:])
    lengths[dim] *= blocks.shape[0]
    return jnp.moveaxis(blocks, 0, dim).reshape(lengths)


def exchange_both(x, axis, axes, splits, concats):
    sizes = [lax.axis_size(a) for a in axes]
    blocks = split_up(x, splits[0], sizes[0])
    blocks = jnp.moveaxis(split_up(blocks, splits[1] + 1, sizes[1]), 0, 1)
    inside = blocks.shape[2:]
    blocks = blocks.reshape(-1, *inside)
    blocks = lax.all_to_all(blocks, axis, split_axis=0, concat_axis=0, tiled=True)
    blocks = in_order(blocks.reshape(*sizes, *inside), concats[0] + 1)
    return in_order(blocks, concats[1])


def sent_together(arrays, axis, dim, along):
    widths = [a.shape[along] for a in arrays]
    both = jnp.concatenate(arrays, axis=along)
    filled = lax.all_gather(both, axis, axis=dim, tiled=True)
    return tuple(jnp.split(filled, [sum(widths[:k]) for k in range(1, len(widths))], axis=along))


def rotate(vectors, positions):
    half_dim = vectors.shape[-1] // 2
    frequency = 1000000.0 ** (-jnp.arange(half_dim, dtype=jnp.float32) / half_dim)
    angles = positions.astype(jnp.float32)[:, None, None] * frequency[None, None, :]
    cosine = jnp.cos(angles)
    sine_part = jnp.sin(angles)
    lower_half = vectors[..., :half_dim]
    upper_half = vectors[..., half_dim:]
    return jnp.concatenate(
        [
            lower_half * cosine - upper_half * sine_part,
            upper_half * cosine + lower_half * sine_part,
        ],
        axis=-1,
    )


def sum_hidden(partial_value):
    return lax.psum_scatter(partial_value, "tp", scatter_dimension=1, tiled=True).astype(
        jnp.bfloat16
    )


def project_strips(merger_hidden, merger_out):
    return jnp.dot(
        lax.all_gather(merger_hidden, ("role", "seq"), axis=0, tiled=True),
        merger_out,
        preferred_element_type=jnp.float32,
    )


def body(
    merger_hidden,
    merger_out,
    row_position,
    prompt_embeds,
    norm_gain,
    query_weight,
    key_weight,
    value_weight,
):
    groups = lax.axis_size("role") * lax.axis_size("seq")
    device_rank = lax.axis_index(("role", "seq"))
    row_count = merger_hidden.shape[0]
    tok_count = prompt_embeds.shape[0]
    columns = prompt_embeds.shape[1]
    model_width = columns * lax.axis_size("tp")
    capacity = 2 * row_count // groups
    strips = project_strips(merger_hidden, merger_out)
    partial_value = lax.all_to_all(strips, ("role", "seq"), split_axis=0, concat_axis=1, tiled=True)
    embeds = sum_hidden(partial_value)
    owners = jnp.where(row_position >= 0, row_position // tok_count, groups)
    onehot = (owners[:, None] == jnp.arange(groups, dtype=jnp.int32)[None, :]).astype(jnp.int32)
    earlier = jnp.sum((jnp.cumsum(onehot, axis=0) - onehot) * onehot, axis=1)
    buffer_slot = jnp.where(owners < groups, owners * capacity + earlier, groups * capacity)
    source = (
        jnp.full((groups * capacity,), row_count, jnp.int32)
        .at[buffer_slot]
        .set(jnp.arange(row_count, dtype=jnp.int32), mode="drop")
    )
    padded = jnp.concatenate([embeds, jnp.zeros((1, columns), jnp.bfloat16)], axis=0)
    outgoing = padded[source].reshape(groups, capacity, columns)
    outgoing_pos = jnp.concatenate([row_position, jnp.full((1,), -1, jnp.int32)])[source].reshape(
        groups, capacity
    )
    role_count = lax.axis_size("role")
    seq_count = lax.axis_size("seq")
    arrived, arrived_pos = (
        exchange_both(
            outgoing.reshape(role_count, seq_count, capacity, columns),
            ("role", "seq"),
            ("role", "seq"),
            (0, 1),
            (0, 1),
        ),
        exchange_both(
            outgoing_pos.reshape(role_count, seq_count, capacity),
            ("role", "seq"),
            ("role", "seq"),
            (0, 1),
            (0, 1),
        ),
    )
    arrived_pos = arrived_pos.reshape(-1)
    local_row = jnp.where(arrived_pos >= 0, arrived_pos - device_rank * tok_count, tok_count)
    stream = prompt_embeds.at[local_row].set(arrived.reshape(-1, columns), mode="drop")
    widened = stream.astype(jnp.float32)
    squares = lax.psum(jnp.sum(widened * widened, axis=1), "tp")
    inverse = lax.rsqrt(squares / model_width + 1e-06)[:, None]
    normed = (widened * inverse * norm_gain.astype(jnp.float32)[None, :]).astype(jnp.bfloat16)
    tables = (query_weight, key_weight, value_weight)
    shard_piece = lax.all_gather(normed, "tp", axis=1, tiled=True)
    query_sum, key_sum, value_sum = tuple(
        (jnp.dot(shard_piece, table, preferred_element_type=jnp.float32) for table in tables)
    )
    local_heads = query_weight.shape[1] // HEAD_DIM
    local_kv = key_weight.shape[1] // HEAD_DIM
    group_size = local_heads // local_kv
    positions = device_rank * tok_count + jnp.arange(tok_count, dtype=jnp.int32)
    queries = rotate(query_sum.reshape(tok_count, local_heads, HEAD_DIM), positions).astype(
        jnp.bfloat16
    )
    queries = queries.reshape(tok_count, local_kv, group_size, HEAD_DIM)
    key_rows = rotate(key_sum.reshape(tok_count, local_kv, HEAD_DIM), positions).astype(
        jnp.bfloat16
    )
    value_rows = value_sum.astype(jnp.bfloat16).reshape(tok_count, local_kv, HEAD_DIM)
    score_scale = 1.0 / math.sqrt(HEAD_DIM)
    running_max = jnp.full((local_kv, group_size, tok_count), -1e30, jnp.float32)
    key_piece, value_piece = sent_together((key_rows, value_rows), ("role", "seq"), 0, 1)
    scores = (
        jnp.einsum("qhgd,khd->hgqk", queries, key_piece, preferred_element_type=jnp.float32)
        * score_scale
    )
    key_pos = jnp.arange(key_piece.shape[0], dtype=jnp.int32)
    visible = key_pos[None, :] <= positions[:, None]
    scores = jnp.where(visible, scores, -jnp.inf)
    next_max = jnp.maximum(running_max, jnp.max(scores, axis=3))
    probability = jnp.where(visible, jnp.exp(scores - next_max[..., None]), 0.0)
    running_sum = jnp.sum(probability, axis=3)
    running_out = jnp.einsum(
        "hgqk,khd->hgqd",
        probability.astype(jnp.bfloat16),
        value_piece,
        preferred_element_type=jnp.float32,
    )
    running_max, running_sum, running_out = (next_max, running_sum, running_out)
    context = running_out / running_sum[..., None]
    context = (
        jnp.transpose(context, (2, 0, 1, 3))
        .reshape(tok_count, local_heads * HEAD_DIM)
        .astype(jnp.bfloat16)
    )
    return (stream, context)


def solution(mesh):
    in_specs = (
        P(("role", "seq"), "tp"),
        P("tp", ("role", "seq")),
        P(("role", "seq")),
        P(("role", "seq"), "tp"),
        P("tp"),
        P(None, "tp"),
        P(None, "tp"),
        P(None, "tp"),
    )
    out_specs = (P(("role", "seq"), "tp"), P(("role", "seq"), "tp"))
    return jax.shard_map(body, mesh=mesh, in_specs=in_specs, out_specs=out_specs, check_vma=False)
```

profile of v0, /device:TPU:97, one launch (start us, length us, event | category | flops | bytes accessed | tf_op | source)
XLA Modules:
  0.0 345.4 jit_solution(12780545009831213138)
XLA Ops:
  8.0 51.0 %all-gather.4.cloned.1.call-done = bf16[2048,1280]{1,0:T(8,128)(2,1)} async-done(((bf16[64,1280]{1,0:T(8,128)(2,1)}), bf16[2048,1280]{1,0:T(8,128)(2,1)}) %all-gather.4.cloned.1.call-update) | async-done | bytes 5242896 | tf_op jit(solution)/shard_map/all_gather | solution.py:65
  59.0 4.2 %fusion.35 = f32[2048,256]{1,0:T(8,128)S(1)} fusion(bf16[2048,1280]{1,0:T(8,128)(2,1)} %all-gather.4.cloned.1.call-done, bf16[1280,256]{1,0:T(8,128)(2,1)} %param.9), kind=kOutput, calls=%fused_computation.73 | convolution fusion | flops 1342177280 | bytes 7995392 | tf_op jit(solution)/shard_map/dot_general | solution.py:64
  63.2 32.4 %all_to_all.29 = f32[32,64,256]{2,1,0:T(8,128)S(1)} all-to-all(f32[32,64,256]{2,1,0:T(8,128)S(1)} %bitcast.88), channel_id=1, replica_groups=mesh['role'=2,'seq'=16,'tp'=4] {'role','seq'}, dimensions={0} | all-to-all | bytes 4194304 | tf_op jit(solution)/shard_map/all_to_all | solution.py:89
  95.6 1.5 copy.49
  98.4 1.2 gather_fusion
  100.4 6.1 %all-to-all-start = ((s32[32,1,1,4]{3,2,1,0:T(1,128)}), s32[32,1,1,4]{3,2,1,0:T(1,128)S(1)}, u32[]{:S(2)}, u32[]{:S(2)}) async-start(s32[32,1,1,4]{3,2,1,0:T(1,128)} %bitcast), calls=%async_computation | async-start | bytes 32768 | tf_op jit(solution)/shard_map/all_to_all | solution.py:28
  106.4 19.6 %reduce-scatter.2.cloned.1.call-done = f32[64,2048]{1,0:T(8,128)} async-done(((f32[64,8192]{1,0:T(8,128)}), f32[64,2048]{1,0:T(8,128)}) %reduce-scatter.2.cloned.1.call-update) | async-done | bytes 524304 | tf_op jit(solution)/shard_map/reduce_scatter | solution.py:58
  127.2 1.7 gather_fusion.1
  128.9 2.0 reshape_transpose_transpose_reshape_reshape_reshape_reshape.7
  130.9 7.7 %all-to-all-start.2 = ((bf16[32,1,1,4,2048]{4,3,2,1,0:T(4,128)(2,1)}), bf16[32,1,1,4,2048]{4,3,2,1,0:T(4,128)(2,1)}, u32[]{:S(2)}, u32[]{:S(2)}) async-start(bf16[32,1,1,4,2048]{4,3,2,1,0:T(4,128)(2,1)} %bitcast.89), calls=%async_computation.3 | async-start | bytes 1048576 | tf_op jit(solution)/shard_map/all_to_all | solution.py:28
  139.0 9.4 %all-to-all-done.2 = bf16[32,1,1,4,2048]{4,3,2,1,0:T(4,128)(2,1)} async-done(((bf16[32,1,1,4,2048]{4,3,2,1,0:T(4,128)(2,1)}), bf16[32,1,1,4,2048]{4,3,2,1,0:T(4,128)(2,1)}, u32[]{:S(2)}, u32[]{:S(2)}) %all-to-all-start.2) | async-done | bytes 524320 | tf_op jit(solution)/shard_map/all_to_all | solution.py:28
  148.4 2.0 reshape.301
  150.3 2.4 scatter_fusion
  153.1 6.6 %psum.7 = f32[256]{0:T(256)S(1)} all-reduce(f32[256]{0:T(256)S(1)} %fusion.7), channel_id=1, replica_groups=mesh['role'=2,'seq'=16,'tp'=4] {'tp'}, use_global_device_ids=true, to_apply=%region_6.7 | all-reduce | flops 256 | bytes 2048 | tf_op jit(solution)/shard_map/psum | solution.py:127
  159.7 1.3 fusion.9
  161.0 47.6 %all-gather.6.cloned.1.call-done = bf16[256,8192]{1,0:T(8,128)(2,1)} async-done(((bf16[256,2048]{1,0:T(8,128)(2,1)}), bf16[256,8192]{1,0:T(8,128)(2,1)}) %all-gather.6.cloned.1.call-update) | async-done | bytes 4194320 | tf_op jit(solution)/shard_map/all_gather | solution.py:131
  208.7 3.8 %convolution_bitcast_fusion.1 = f32[256,1,128]{0,2,1:T(8,128)S(1)} fusion(bf16[256,8192]{1,0:T(8,128)(2,1)} %all-gather.6.cloned.1.call-done, bf16[8192,128]{1,0:T(8,128)(2,1)S(1)} %copy-done), kind=kOutput, calls=%fused_computation.22 | convolution fusion | flops 536870912 | bytes 6422528 | tf_op jit(solution)/shard_map/dot_general | solution.py:133
  212.9 1.5 fusion.11
  215.6 2.7 iota_compare_fusion
  218.4 9.5 %convolution_bitcast_fusion = f32[32,8,8,128]{3,1,2,0:T(8,128)S(1)} fusion(bf16[256,8192]{1,0:T(8,128)(2,1)} %all-gather.6.cloned.1.call-done, bf16[8192,1024]{1,0:T(8,128)(2,1)} %param.13), kind=kOutput, calls=%fused_computation.21 | convolution fusion | flops 4294967296 | bytes 22020096 | tf_op jit(solution)/shard_map/dot_general | solution.py:133
  228.8 36.0 %all-gather.8.cloned.1.call-done = bf16[8192,2,128]{0,2,1:T(8,128)(2,1)} async-done(((bf16[256,2,128]{0,2,1:T(8,128)(2,1)}), bf16[8192,2,128]{0,2,1:T(8,128)(2,1)}) %all-gather.8.cloned.1.call-update) | async-done | bytes 4194320 | tf_op jit(solution)/shard_map/all_gather | solution.py:36
  264.9 25.4 %fusion = (f32[8,256]{1,0:T(8,128)S(1)}, f32[8192,256,8]{1,0,2:T(8,128)}) fusion(pred[256,8192]{0,1:T(8,128)(4,1)} %iota_compare_fusion, bf16[256,8,64]{2,0,1:T(8,128)(2,1)S(1)} %get-tuple-element.9, bf16[256,8,64]{2,0,1:T(8,128)(2,1)S(1)} %get-tuple-element.8, bf16[8192,2,128]{0,2,1:T(8,128)(2,1)} %all-gather.8.cloned.1.call-done), kind=kOutput, calls=%fused_computation.6 | convolution fusion | flops 4346345472 | bytes 71835648 | tf_op jit(solution)/shard_map/qhgd,khd->hgqk/dot_general | solution.py:151
  290.3 22.3 %fusion.1 = f32[8,256]{1,0:T(8,128)S(1)} fusion(f32[8192,256,8]{1,0,2:T(8,128)} %get-tuple-element.17, f32[8,256]{1,0:T(8,128)S(1)} %broadcast_maximum_fusion, pred[256,8192]{0,1:T(8,128)(4,1)} %iota_compare_fusion), kind=kLoop, calls=%fused_computation.7 | loop fusion | flops 83884032 | bytes 69222400 | tf_op jit(solution)/shard_map/reduce_sum | solution.py:159
  312.5 25.3 %divide_convert_fusion = bf16[8,256,128]{1,2,0:T(8,128)(2,1)S(1)} fusion(f32[8192,256,8]{1,0,2:T(8,128)} %get-tuple-element.17, f32[8,256]{1,0:T(8,128)S(1)} %broadcast_maximum_fusion, pred[256,8192]{0,1:T(8,128)(4,1)} %iota_compare_fusion, bf16[8192,2,128]{0,2,1:T(8,128)(2,1)} %all-gather.8.cloned.1.call-done, f32[8,256]{1,0:T(8,128)S(1)} %fusion.1), kind=kOutput, calls=%fused_computation.25 | convolution fusion | flops 4379377664 | bytes 71843840 | tf_op jit(solution)/shard_map/hgqk,khd->hgqd/dot_general | solution.py:160
  (56 shorter events, 8.1 us)
Async XLA Ops:
  7.2 201.5 %copy-start = (bf16[8192,128]{1,0:T(8,128)(2,1)S(1)}, bf16[8192,128]{1,0:T(8,128)(2,1)}, u32[]{:S(2)}) copy-start(bf16[8192,128]{1,0:T(8,128)(2,1)} %param.14) | copy-start | bytes 6291460
  7.2 51.8 %all-gather.4.cloned.1.call-start = ((), (), s32[]{:S(2)}) async-start(), calls=%async_computation.4 | async-start | bytes 5406720 | tf_op jit(solution)/shard_map/all_gather | solution.py:65
  7.9 118.1 %reduce-scatter.2.cloned.1.call-start = ((), (), s32[]{:S(2)}) async-start(), calls=%async_computation.5 | async-start | bytes 2621440 | tf_op jit(solution)/shard_map/reduce_scatter | solution.py:58
  95.6 1.5 copy-start.6
  99.6 39.0 %copy-start.5 = (bf16[2048]{0:T(1024)(128)(2,1)S(1)}, bf16[2048]{0:T(1024)(128)(2,1)}, u32[]{:S(2)}) copy-start(bf16[2048]{0:T(1024)(128)(2,1)} %param.12) | copy-start | bytes 12292
  100.4 30.6 %all-to-all-start = ((s32[32,1,1,4]{3,2,1,0:T(1,128)}), s32[32,1,1,4]{3,2,1,0:T(1,128)S(1)}, u32[]{:S(2)}, u32[]{:S(2)}) async-start(s32[32,1,1,4]{3,2,1,0:T(1,128)} %bitcast), calls=%async_computation | async-start | bytes 32768 | tf_op jit(solution)/shard_map/all_to_all | solution.py:28
  127.1 23.2 %copy-start.2 = (bf16[256,2048]{1,0:T(8,128)(2,1)S(1)}, bf16[256,2048]{1,0:T(8,128)(2,1)}, u32[]{:S(2)}) copy-start(bf16[256,2048]{1,0:T(8,128)(2,1)} %param.11) | copy-start | bytes 3145732
  130.9 17.5 %all-to-all-start.2 = ((bf16[32,1,1,4,2048]{4,3,2,1,0:T(4,128)(2,1)}), bf16[32,1,1,4,2048]{4,3,2,1,0:T(4,128)(2,1)}, u32[]{:S(2)}, u32[]{:S(2)}) async-start(bf16[32,1,1,4,2048]{4,3,2,1,0:T(4,128)(2,1)} %bitcast.89), calls=%async_computation.3 | async-start | bytes 1048576 | tf_op jit(solution)/shard_map/all_to_all | solution.py:28
  138.6 70.1 %all-gather.6.cloned.1.call-start = ((), (), s32[]{:S(2)}) async-start(), calls=%async_computation.6 | async-start | bytes 5242880 | tf_op jit(solution)/shard_map/all_gather | solution.py:131
  152.8 59.8 %copy-start.1 = (bf16[256,2048]{1,0:T(8,128)(2,1)}, bf16[256,2048]{1,0:T(8,128)(2,1)S(1)}, u32[]{:S(2)}) copy-start(bf16[256,2048]{1,0:T(8,128)(2,1)S(1)} %scatter_fusion) | copy-start | bytes 3145732
  161.0 103.9 %all-gather.8.cloned.1.call-start = ((), (), s32[]{:S(2)}) async-start(), calls=%async_computation.7 | async-start | bytes 4325376 | tf_op jit(solution)/shard_map/all_gather | solution.py:36
  208.7 4.2 %copy-start.3 = (bf16[256,8192]{1,0:T(8,128)(2,1)S(1)}, bf16[256,8192]{1,0:T(8,128)(2,1)}, u32[]{:S(2)}) copy-start(bf16[256,8192]{1,0:T(8,128)(2,1)} %all-gather.6.cloned.1.call-done) | copy-start | bytes 12582916
  208.7 4.2 %copy-start.4 = (bf16[8192,128]{1,0:T(8,128)(2,1)S(1)}, bf16[8192,128]{1,0:T(8,128)(2,1)}, u32[]{:S(2)}) copy-start(bf16[8192,128]{1,0:T(8,128)(2,1)} %param.15) | copy-start | bytes 6291460
Sparse Core Ops, SparseCore 0:
  10.3 48.6 all-gather.3
  97.2 28.7 reduce-scatter.1
  161.1 47.5 all-gather.5
  215.2 49.5 all-gather.7
where the time goes:
time: 348 us; the launch traced here: 345 us
  waiting for transfers between devices  164 us (47%)
  matrix products  69.8 us (20%)
  blocking collectives  39 us (11%)
  other arithmetic  30.1 us (9%)
  local copies, waits for them, and re-layouts  14.2 us (4%)
  between operations  14.1 us (4%)
  starting transfers between devices  13.9 us (4%)
    all_gather x1, waiting for transfers between devices, project_strips(): lax.all_gather(merger_hidden, ('role', 'seq'), axis=0, tiled=True)  51 us
    all_gather x1, waiting for transfers between devices, body(): shard_piece = lax.all_gather(normed, 'tp', axis=1, tiled=True)  47.6 us
    all_gather x1, waiting for transfers between devices, sent_together(): filled = lax.all_gather(both, axis, axis=dim, tiled=True)  36 us
    all_to_all x1, blocking collectives, body(): lax.all_to_all(strips, ('role', 'seq'), split_axis=0, concat_axis=1, tile...  32.4 us
    dot_general x1, matrix products, body(): jnp.einsum('qhgd,khd->hgqk', queries, key_piece, preferred_element_type=j...  25.4 us
    dot_general x1, matrix products, body(): jnp.einsum('hgqk,khd->hgqd', probability.astype(jnp.bfloat16), value_piec...  25.3 us
    reduce_sum x1, other arithmetic, body(): running_sum = jnp.sum(probability, axis=3)  22.3 us
    reduce_scatter x1, waiting for transfers between devices, sum_hidden(): lax.psum_scatter(partial_value, 'tp', scatter_dimension=1, tiled=True)  19.6 us
  transfers between devices with their start and end apart: 6, of which 5 were waited for; matrix products, arithmetic and copies ran while one was open for 6% of the time, Pallas kernels for 0%

commit v1 on v0

--- a/solution.py
+++ b/solution.py
@@ -1,8 +1,11 @@
+import functools
 import math
 
 import jax
 import jax.numpy as jnp
 from jax import lax
+from jax.experimental import pallas as pl
+from jax.experimental.pallas import tpu as pltpu
 from jax.sharding import PartitionSpec as P
 
 HEAD_DIM = 128
@@ -66,6 +69,70 @@
         merger_out,
         preferred_element_type=jnp.float32,
     )
+
+
+KEY_BLOCK = 1024
+
+
+def attend_kernel(heads, q_ref, k_ref, v_ref, o_ref, acc, top, total):
+    rows = q_ref.shape[0]
+    first = (lax.axis_index("role") * lax.axis_size("seq") + lax.axis_index("seq")) * rows
+    factor = math.log2(math.e) / math.sqrt(HEAD_DIM)
+    acc[...] = jnp.zeros_like(acc)
+    total[...] = jnp.zeros_like(total)
+    top[...] = jnp.full_like(top, -1e30)
+
+    def block(b, masked):
+        start = pl.multiple_of(b * KEY_BLOCK, KEY_BLOCK)
+        k = k_ref[pl.ds(start, KEY_BLOCK), :]
+        v = v_ref[pl.ds(start, KEY_BLOCK), :]
+        if masked:
+            key_pos = start + lax.broadcasted_iota(jnp.int32, (rows, KEY_BLOCK), 1)
+            query_pos = first + lax.broadcasted_iota(jnp.int32, (rows, KEY_BLOCK), 0)
+            visible = key_pos <= query_pos
+        for h in range(heads):
+            q = q_ref[:, h * HEAD_DIM : (h + 1) * HEAD_DIM]
+            s = lax.dot_general(
+                q, k, (((1,), (1,)), ((), ())), preferred_element_type=jnp.float32
+            )
+            if masked:
+                s = jnp.where(visible, s, -1e30)
+            old = top[h][:, :1]
+            new = jnp.maximum(old, jnp.max(s, axis=1, keepdims=True))
+            p = jnp.exp2((s - new) * factor)
+            alpha = jnp.exp2((old - new) * factor)
+            part = p[:, :HEAD_DIM]
+            for c in range(1, KEY_BLOCK // HEAD_DIM):
+                part = part + p[:, c * HEAD_DIM : (c + 1) * HEAD_DIM]
+            total[h] = total[h] * alpha + part
+            acc[h] = acc[h] * alpha + jnp.dot(
+                p.astype(jnp.bfloat16), v, preferred_element_type=jnp.float32
+            )
+            top[h] = jnp.broadcast_to(new, (rows, HEAD_DIM))
+
+    full = first // KEY_BLOCK
+
+    @pl.loop(0, full)
+    def _(b):
+        block(b, False)
+
+    block(full, True)
+    for h in range(heads):
+        l = jnp.sum(total[h], axis=1, keepdims=True)
+        o_ref[:, h * HEAD_DIM : (h + 1) * HEAD_DIM] = (acc[h] / l).astype(o_ref.dtype)
+
+
+def attend(q, k, v, heads):
+    rows = q.shape[0]
+    vmem = pl.BlockSpec(memory_space=pltpu.VMEM)
+    return pl.pallas_call(
+        functools.partial(attend_kernel, heads),
+        out_shape=jax.ShapeDtypeStruct(q.shape, jnp.bfloat16),
+        in_specs=[vmem] * 3,
+        out_specs=vmem,
+        scratch_shapes=[pltpu.VMEM((heads, rows, HEAD_DIM), jnp.float32)] * 3,
+        compiler_params=pltpu.CompilerParams(vmem_limit_bytes=48 << 20),
+    )(q, k, v)
 
 
 def body(
@@ -134,41 +201,20 @@
     )
     local_heads = query_weight.shape[1] // HEAD_DIM
     local_kv = key_weight.shape[1] // HEAD_DIM
-    group_size = local_heads // local_kv
     positions = device_rank * tok_count + jnp.arange(tok_count, dtype=jnp.int32)
     queries = rotate(query_sum.reshape(tok_count, local_heads, HEAD_DIM), positions).astype(
         jnp.bfloat16
     )
-    queries = queries.reshape(tok_count, local_kv, group_size, HEAD_DIM)
     key_rows = rotate(key_sum.reshape(tok_count, local_kv, HEAD_DIM), positions).astype(
         jnp.bfloat16
     )
     value_rows = value_sum.astype(jnp.bfloat16).reshape(tok_count, local_kv, HEAD_DIM)
-    score_scale = 1.0 / math.sqrt(HEAD_DIM)
-    running_max = jnp.full((local_kv, group_size, tok_count), -1e30, jnp.float32)
     key_piece, value_piece = sent_together((key_rows, value_rows), ("role", "seq"), 0, 1)
-    scores = (
-        jnp.einsum("qhgd,khd->hgqk", queries, key_piece, preferred_element_type=jnp.float32)
-        * score_scale
-    )
-    key_pos = jnp.arange(key_piece.shape[0], dtype=jnp.int32)
-    visible = key_pos[None, :] <= positions[:, None]
-    scores = jnp.where(visible, scores, -jnp.inf)
-    next_max = jnp.maximum(running_max, jnp.max(scores, axis=3))
-    probability = jnp.where(visible, jnp.exp(scores - next_max[..., None]), 0.0)
-    running_sum = jnp.sum(probability, axis=3)
-    running_out = jnp.einsum(
-        "hgqk,khd->hgqd",
-        probability.astype(jnp.bfloat16),
-        value_piece,
-        preferred_element_type=jnp.float32,
-    )
-    running_max, running_sum, running_out = (next_max, running_sum, running_out)
-    context = running_out / running_sum[..., None]
-    context = (
-        jnp.transpose(context, (2, 0, 1, 3))
-        .reshape(tok_count, local_heads * HEAD_DIM)
-        .astype(jnp.bfloat16)
+    context = attend(
+        queries.reshape(tok_count, local_heads * HEAD_DIM),
+        key_piece.reshape(-1, HEAD_DIM),
+        value_piece.reshape(-1, HEAD_DIM),
+        local_heads,
     )
     return (stream, context)
 

time: 348 us -> 311 us (0.89)
  matrix products: 69.8 us -> 18.4 us
  Pallas kernels: 0 us -> 40 us
  other arithmetic: 30.1 us -> 5.83 us
    dot_general x2 -> x0, matrix products: 50.7 us -> none  [the longest x1 25.4 us: body(): jnp.einsum('qhgd,khd->hgqk', queries, key_piece, preferred_element_type=j...]
    pallas_call x0 -> x1, Pallas kernels: none -> 40 us  [attend(): pl.pallas_call(functools.partial(attend_kernel, heads), out_shape=jax.Sha...]
    reduce_sum x1 -> x0, other arithmetic: 22.3 us -> none  [body(): running_sum = jnp.sum(probability, axis=3)]
where the time goes in v1:
time: 311 us
  waiting for transfers between devices  163 us (52%)
  Pallas kernels  40 us (13%)
  blocking collectives  39 us (13%)
  matrix products  18.4 us (6%)
  local copies, waits for them, and re-layouts  16.2 us (5%)
  starting transfers between devices  14 us (5%)
  between operations  14 us (5%)
  other arithmetic  5.83 us (2%)
    all_gather x1, waiting for transfers between devices, project_strips(): lax.all_gather(merger_hidden, ('role', 'seq'), axis=0, tiled=True)  51 us
    all_gather x1, waiting for transfers between devices, body(): shard_piece = lax.all_gather(normed, 'tp', axis=1, tiled=True)  47.4 us
    pallas_call x1, Pallas kernels, attend(): pl.pallas_call(functools.partial(attend_kernel, heads), out_shape=jax.Sha...  40 us
    all_gather x1, waiting for transfers between devices, sent_together(): filled = lax.all_gather(both, axis, axis=dim, tiled=True)  35.6 us
    all_to_all x1, blocking collectives, body(): lax.all_to_all(strips, ('role', 'seq'), split_axis=0, concat_axis=1, tile...  32.4 us
    reduce_scatter x1, waiting for transfers between devices, sum_hidden(): lax.psum_scatter(partial_value, 'tp', scatter_dimension=1, tiled=True)  19.1 us
    dot_general x3, matrix products, body(): jnp.dot(shard_piece, table, preferred_element_type=jnp.float32)  14.3 us
    all_to_all x2, starting transfers between devices, exchange_both(): lax.all_to_all(blocks, axis, split_axis=0, concat_axis=0, tiled=True)  13.7 us
  transfers between devices with their start and end apart: 6, of which 5 were waited for; matrix products, arithmetic and copies ran while one was open for 6% of the time, Pallas kernels for 0%

profile of v1, /device:TPU:97, one launch (start us, length us, event | category | flops | bytes accessed | tf_op | source)
XLA Modules:
  0.0 310.7 jit_solution(17708886500104351293)
XLA Ops:
  8.0 51.0 %all-gather.4.cloned.1.call-done = bf16[2048,1280]{1,0:T(8,128)(2,1)} async-done(((bf16[64,1280]{1,0:T(8,128)(2,1)}), bf16[2048,1280]{1,0:T(8,128)(2,1)}) %all-gather.4.cloned.1.call-update) | async-done | bytes 5242896 | tf_op jit(solution)/shard_map/all_gather | solution.py:68
  59.0 4.1 %fusion.16 = f32[2048,256]{1,0:T(8,128)S(1)} fusion(bf16[2048,1280]{1,0:T(8,128)(2,1)} %all-gather.4.cloned.1.call-done, bf16[1280,256]{1,0:T(8,128)(2,1)S(1)} %copy-done.6), kind=kOutput, calls=%fused_computation.54 | convolution fusion | flops 1342177280 | bytes 7995392 | tf_op jit(solution)/shard_map/dot_general | solution.py:67
  63.0 32.4 %all_to_all.29 = f32[32,64,256]{2,1,0:T(8,128)S(1)} all-to-all(f32[32,64,256]{2,1,0:T(8,128)S(1)} %bitcast.58), channel_id=1, replica_groups=mesh['role'=2,'seq'=16,'tp'=4] {'role','seq'}, dimensions={0} | all-to-all | bytes 4194304 | tf_op jit(solution)/shard_map/all_to_all | solution.py:156
  95.4 1.5 copy.37
  98.0 0.8 scatter_custom_fusion
  98.9 1.2 gather_fusion
  100.8 6.1 %all-to-all-start = ((s32[32,1,1,4]{3,2,1,0:T(1,128)}), s32[32,1,1,4]{3,2,1,0:T(1,128)S(1)}, u32[]{:S(2)}, u32[]{:S(2)}) async-start(s32[32,1,1,4]{3,2,1,0:T(1,128)} %bitcast), calls=%async_computation | async-start | bytes 32768 | tf_op jit(solution)/shard_map/all_to_all | solution.py:31
  106.9 19.1 %reduce-scatter.2.cloned.1.call-done = f32[64,2048]{1,0:T(8,128)} async-done(((f32[64,8192]{1,0:T(8,128)}), f32[64,2048]{1,0:T(8,128)}) %reduce-scatter.2.cloned.1.call-update) | async-done | bytes 524304 | tf_op jit(solution)/shard_map/reduce_scatter | solution.py:61
  126.0 1.1 convert_element_type.41
  127.1 1.7 gather_fusion.1
  128.8 2.1 reshape_transpose_transpose_reshape_reshape_reshape_reshape.7
  130.9 7.6 %all-to-all-start.2 = ((bf16[32,1,1,4,2048]{4,3,2,1,0:T(4,128)(2,1)}), bf16[32,1,1,4,2048]{4,3,2,1,0:T(4,128)(2,1)}, u32[]{:S(2)}, u32[]{:S(2)}) async-start(bf16[32,1,1,4,2048]{4,3,2,1,0:T(4,128)(2,1)} %bitcast.59), calls=%async_computation.3 | async-start | bytes 1048576 | tf_op jit(solution)/shard_map/all_to_all | solution.py:31
  139.0 9.4 %all-to-all-done.2 = bf16[32,1,1,4,2048]{4,3,2,1,0:T(4,128)(2,1)} async-done(((bf16[32,1,1,4,2048]{4,3,2,1,0:T(4,128)(2,1)}), bf16[32,1,1,4,2048]{4,3,2,1,0:T(4,128)(2,1)}, u32[]{:S(2)}, u32[]{:S(2)}) %all-to-all-start.2) | async-done | bytes 524320 | tf_op jit(solution)/shard_map/all_to_all | solution.py:31
  148.4 2.0 reshape.266
  150.3 2.4 scatter_fusion
  153.0 6.6 %psum.7 = f32[256]{0:T(256)S(1)} all-reduce(f32[256]{0:T(256)S(1)} %fusion), channel_id=1, replica_groups=mesh['role'=2,'seq'=16,'tp'=4] {'tp'}, use_global_device_ids=true, to_apply=%region_6.7 | all-reduce | flops 256 | bytes 2048 | tf_op jit(solution)/shard_map/psum | solution.py:194
  159.6 1.3 fusion.2
  161.2 47.4 %all-gather.6.cloned.1.call-done = bf16[256,8192]{1,0:T(8,128)(2,1)} async-done(((bf16[256,2048]{1,0:T(8,128)(2,1)}), bf16[256,8192]{1,0:T(8,128)(2,1)}) %all-gather.6.cloned.1.call-update) | async-done | bytes 4194320 | tf_op jit(solution)/shard_map/all_gather | solution.py:198
  208.6 3.6 %convolution_bitcast_fusion.1 = f32[256,1,128]{2,0,1:T(8,128)S(1)} fusion(bf16[256,8192]{1,0:T(8,128)(2,1)} %all-gather.6.cloned.1.call-done, bf16[8192,128]{1,0:T(8,128)(2,1)S(1)} %copy-done), kind=kOutput, calls=%fused_computation.12 | convolution fusion | flops 536870912 | bytes 6422528 | tf_op jit(solution)/shard_map/dot_general | solution.py:200
  212.9 1.2 fusion.3
  215.5 9.4 %convolution_bitcast_fusion = f32[32,8,8,128]{3,1,2,0:T(8,128)S(1)} fusion(bf16[256,8192]{1,0:T(8,128)(2,1)} %all-gather.6.cloned.1.call-done, bf16[8192,1024]{1,0:T(8,128)(2,1)} %param.13), kind=kOutput, calls=%fused_computation.11 | convolution fusion | flops 4294967296 | bytes 22020096 | tf_op jit(solution)/shard_map/dot_general | solution.py:200
  226.1 35.6 %all-gather.8.cloned.1.call-done = bf16[8192,2,128]{2,0,1:T(8,128)(2,1)} async-done(((bf16[256,2,128]{2,0,1:T(8,128)(2,1)}), bf16[8192,2,128]{2,0,1:T(8,128)(2,1)}) %all-gather.8.cloned.1.call-update) | async-done | bytes 4194320 | tf_op jit(solution)/shard_map/all_gather | solution.py:39
  261.7 2.5 slice_bitcast_fusion
  264.2 40.0 %shard_map.95 = bf16[256,1024]{1,0:T(8,128)(2,1)} custom-call(bf16[256,1024]{1,0:T(8,128)(2,1)S(1)} %bitcast.53, bf16[8192,128]{1,0:T(8,128)(2,1)S(1)} %get-tuple-element.3.k_ref, bf16[8192,128]{1,0:T(8,128)(2,1)S(1)} %get-tuple-element.2.v_ref), custom_call_target="tpu_custom_call" | custom-call | tf_op jit(solution)/shard_map/pallas_call | solution.py:128
  (54 shorter events, 6.5 us)
Async XLA Ops:
  7.2 201.5 %copy-start = (bf16[8192,128]{1,0:T(8,128)(2,1)S(1)}, bf16[8192,128]{1,0:T(8,128)(2,1)}, u32[]{:S(2)}) copy-start(bf16[8192,128]{1,0:T(8,128)(2,1)} %param.14) | copy-start | bytes 6291460
  7.2 51.8 %copy-start.6 = (bf16[1280,256]{1,0:T(8,128)(2,1)S(1)}, bf16[1280,256]{1,0:T(8,128)(2,1)}, u32[]{:S(2)}) copy-start(bf16[1280,256]{1,0:T(8,128)(2,1)} %param.9) | copy-start | bytes 1966084
  7.2 51.8 %all-gather.4.cloned.1.call-start = ((), (), s32[]{:S(2)}) async-start(), calls=%async_computation.4 | async-start | bytes 5406720 | tf_op jit(solution)/shard_map/all_gather | solution.py:68
  7.9 118.0 %reduce-scatter.2.cloned.1.call-start = ((), (), s32[]{:S(2)}) async-start(), calls=%async_computation.5 | async-start | bytes 2621440 | tf_op jit(solution)/shard_map/reduce_scatter | solution.py:61
  97.0 0.7 copy-start.7
  100.8 30.1 %all-to-all-start = ((s32[32,1,1,4]{3,2,1,0:T(1,128)}), s32[32,1,1,4]{3,2,1,0:T(1,128)S(1)}, u32[]{:S(2)}, u32[]{:S(2)}) async-start(s32[32,1,1,4]{3,2,1,0:T(1,128)} %bitcast), calls=%async_computation | async-start | bytes 32768 | tf_op jit(solution)/shard_map/all_to_all | solution.py:31
  128.8 9.8 %copy-start.5 = (bf16[2048]{0:T(1024)(128)(2,1)S(1)}, bf16[2048]{0:T(1024)(128)(2,1)}, u32[]{:S(2)}) copy-start(bf16[2048]{0:T(1024)(128)(2,1)} %param.12) | copy-start | bytes 12292
  128.8 21.5 %copy-start.2 = (bf16[256,2048]{1,0:T(8,128)(2,1)S(1)}, bf16[256,2048]{1,0:T(8,128)(2,1)}, u32[]{:S(2)}) copy-start(bf16[256,2048]{1,0:T(8,128)(2,1)} %param.11) | copy-start | bytes 3145732
  130.9 17.4 %all-to-all-start.2 = ((bf16[32,1,1,4,2048]{4,3,2,1,0:T(4,128)(2,1)}), bf16[32,1,1,4,2048]{4,3,2,1,0:T(4,128)(2,1)}, u32[]{:S(2)}, u32[]{:S(2)}) async-start(bf16[32,1,1,4,2048]{4,3,2,1,0:T(4,128)(2,1)} %bitcast.59), calls=%async_computation.3 | async-start | bytes 1048576 | tf_op jit(solution)/shard_map/all_to_all | solution.py:31
  138.5 70.1 %all-gather.6.cloned.1.call-start = ((), (), s32[]{:S(2)}) async-start(), calls=%async_computation.6 | async-start | bytes 5242880 | tf_op jit(solution)/shard_map/all_gather | solution.py:198
  152.7 8.2 %copy-start.1 = (bf16[256,2048]{1,0:T(8,128)(2,1)}, bf16[256,2048]{1,0:T(8,128)(2,1)S(1)}, u32[]{:S(2)}) copy-start(bf16[256,2048]{1,0:T(8,128)(2,1)S(1)} %scatter_fusion) | copy-start | bytes 3145732
  160.9 100.7 %all-gather.8.cloned.1.call-start = ((), (), s32[]{:S(2)}) async-start(), calls=%async_computation.7 | async-start | bytes 4325376 | tf_op jit(solution)/shard_map/all_gather | solution.py:39
  208.6 4.2 %copy-start.3 = (bf16[256,8192]{1,0:T(8,128)(2,1)S(1)}, bf16[256,8192]{1,0:T(8,128)(2,1)}, u32[]{:S(2)}) copy-start(bf16[256,8192]{1,0:T(8,128)(2,1)} %all-gather.6.cloned.1.call-done) | copy-start | bytes 12582916
  208.6 4.3 %copy-start.4 = (bf16[8192,128]{1,0:T(8,128)(2,1)S(1)}, bf16[8192,128]{1,0:T(8,128)(2,1)}, u32[]{:S(2)}) copy-start(bf16[8192,128]{1,0:T(8,128)(2,1)} %param.15) | copy-start | bytes 6291460
Sparse Core Ops, SparseCore 0:
  10.3 48.6 all-gather.3
  97.1 28.8 reduce-scatter.1
  161.0 47.5 all-gather.5
  215.0 46.5 all-gather.7

commit v2 on v1

--- a/solution.py
+++ b/solution.py
@@ -9,28 +9,6 @@
 from jax.sharding import PartitionSpec as P
 
 HEAD_DIM = 128
-
-
-def split_up(x, dim, length):
-    before, after = (x.shape[:dim], x.shape[dim + 1 :])
-    return jnp.moveaxis(x.reshape(*before, length, -1, *after), dim, 0)
-
-
-def in_order(blocks, dim):
-    lengths = list(blocks.shape[1:])
-    lengths[dim] *= blocks.shape[0]
-    return jnp.moveaxis(blocks, 0, dim).reshape(lengths)
-
-
-def exchange_both(x, axis, axes, splits, concats):
-    sizes = [lax.axis_size(a) for a in axes]
-    blocks = split_up(x, splits[0], sizes[0])
-    blocks = jnp.moveaxis(split_up(blocks, splits[1] + 1, sizes[1]), 0, 1)
-    inside = blocks.shape[2:]
-    blocks = blocks.reshape(-1, *inside)
-    blocks = lax.all_to_all(blocks, axis, split_axis=0, concat_axis=0, tiled=True)
-    blocks = in_order(blocks.reshape(*sizes, *inside), concats[0] + 1)
-    return in_order(blocks, concats[1])
 
 
 def sent_together(arrays, axis, dim, along):
@@ -57,18 +35,289 @@
     )
 
 
-def sum_hidden(partial_value):
-    return lax.psum_scatter(partial_value, "tp", scatter_dimension=1, tiled=True).astype(
-        jnp.bfloat16
-    )
-
-
-def project_strips(merger_hidden, merger_out):
-    return jnp.dot(
-        lax.all_gather(merger_hidden, ("role", "seq"), axis=0, tiled=True),
-        merger_out,
+MESH = pl.DeviceIdType.MESH
+SIDE = 4
+
+
+def remote(src, dst, send_sem, recv_sem, role, seq, tp):
+    return pltpu.make_async_remote_copy(
+        src_ref=src,
+        dst_ref=dst,
+        send_sem=send_sem,
+        recv_sem=recv_sem,
+        device_id=(role, seq, tp),
+        device_id_type=MESH,
+    )
+
+
+def plane_gather(buf, full_sem, half_sem, send_sem, between=()):
+    role, seq, tp = lax.axis_index("role"), lax.axis_index("seq"), lax.axis_index("tp")
+    step_a, step_b = 1 + 3 * role, 4 - 3 * role
+    z, x = seq // SIDE, seq % SIDE
+    ca = x + role * (z - x)
+    cb = z + role * (x - z)
+    half = buf.shape[1] // 2
+    sent = []
+
+    def seq_of(a, b):
+        return ((ca + a + SIDE) % SIDE) * step_a + ((cb + b + SIDE) % SIDE) * step_b
+
+    def slot_of(a, b):
+        return role * (SIDE * SIDE) + seq_of(a, b)
+
+    def whole(slot, to_role, to_seq):
+        copy = remote(
+            buf.at[slot], buf.at[slot], send_sem.at[len(sent)], full_sem.at[slot], to_role, to_seq, tp
+        )
+        copy.start()
+        sent.append(copy)
+
+    def part(slot, k, to_seq):
+        piece = buf.at[slot, pl.ds(k * half, half)]
+        copy = remote(
+            piece, piece, send_sem.at[len(sent)], half_sem.at[slot, k], role, to_seq, tp
+        )
+        copy.start()
+        sent.append(copy)
+
+    def wait_whole(slot):
+        pltpu.make_async_copy(buf.at[slot], buf.at[slot], full_sem.at[slot]).wait()
+
+    def wait_parts(slot):
+        for k in range(2):
+            piece = buf.at[slot, pl.ds(k * half, half)]
+            pltpu.make_async_copy(piece, piece, half_sem.at[slot, k]).wait()
+
+    def spread_b(slot):
+        whole(slot, role, seq_of(0, 1))
+        whole(slot, role, seq_of(0, -1))
+        whole(slot, 1 - role, seq)
+
+    own = slot_of(0, 0)
+    whole(own, role, seq_of(1, 0))
+    whole(own, role, seq_of(-1, 0))
+    spread_b(own)
+    for a, k in ((-1, 0), (1, 1)):
+        wait_whole(slot_of(a, 0))
+        part(slot_of(a, 0), k, seq_of(-a, 0))
+        spread_b(slot_of(a, 0))
+
+    def pass_b(a):
+        for b, k in ((-1, 0), (1, 1)):
+            wait_whole(slot_of(a, b))
+            part(slot_of(a, b), k, seq_of(0, -b))
+            whole(slot_of(a, b), 1 - role, seq)
+
+    pass_b(0)
+    wait_parts(slot_of(2, 0))
+    spread_b(slot_of(2, 0))
+    for a in (-1, 1, 2):
+        pass_b(a)
+    for a in (0, -1, 1, 2):
+        wait_parts(slot_of(a, 2))
+        whole(slot_of(a, 2), 1 - role, seq)
+    for s in range(SIDE * SIDE):
+        wait_whole((1 - role) * (SIDE * SIDE) + s)
+    for copy in sent:
+        copy.wait_send()
+
+
+PLANE_SENDS = 2 + 3 * 4 + 2 + 8 + 12
+
+
+def iota(shape, dim):
+    return lax.broadcasted_iota(jnp.int32, shape, dim).astype(jnp.float32)
+
+
+def merge_kernel(
+    hidden,
+    weight,
+    position,
+    prompt,
+    stream,
+    buf,
+    full_sem,
+    half_sem,
+    send_sem,
+    partial,
+    landed,
+    y_send,
+    y_recv,
+    table,
+    place,
+    packed,
+    arrived,
+    d_send,
+    d_recv,
+):
+    role, seq, tp = lax.axis_index("role"), lax.axis_index("seq"), lax.axis_index("tp")
+    rank = role * lax.axis_size("seq") + seq
+    rows, width = hidden.shape
+    tokens = prompt.shape[0]
+    groups = buf.shape[0]
+    columns = weight.shape[1]
+    capacity = 2 * rows // groups
+    lane = lax.broadcasted_iota(jnp.int32, (rows, 128), 1)
+    pos = jnp.broadcast_to(position[...], (rows, 128))
+    owner = jnp.where(pos >= 0, pos // tokens, -1)
+    rest = jnp.where(pos >= 0, pos % tokens, 0)
+    code = jnp.where(lane == 0, owner, jnp.where(lane == 1, rest, 0))
+    buf[rank, :, :width] = hidden[...]
+    buf[rank, :, width:] = code.astype(jnp.float32).astype(jnp.bfloat16)
+    plane_gather(buf, full_sem, half_sem, send_sem)
+
+    quarter = groups // 4
+    block = quarter * rows
+    copies = []
+    for i, off in enumerate((2, 1, 3, 0)):
+        q = (tp + off) % 4
+        left = buf[pl.ds(q * quarter, quarter), :, :width].reshape(block, width)
+        value = jnp.dot(left, weight[...], preferred_element_type=jnp.float32)
+        if off:
+            partial[i] = value.astype(jnp.bfloat16)
+            copy = remote(
+                partial.at[i], landed.at[off - 1], y_send.at[i], y_recv.at[off - 1], role, seq, q
+            )
+            copy.start()
+            copies.append(copy)
+    mine = value
+
+    some = 256
+    batch = some // rows
+    r0 = lax.broadcasted_iota(jnp.int32, (some, some), 0)
+    r1 = lax.broadcasted_iota(jnp.int32, (some, some), 1)
+    lower = jnp.where((r1 < r0) & (r1 // rows == r0 // rows), 1.0, 0.0).astype(jnp.bfloat16)
+    source = (lax.broadcasted_iota(jnp.int32, (some, 1), 0) // rows).astype(jnp.float32)
+
+    def decode(first):
+        got = buf[pl.ds(first, batch), :, width:].reshape(some, 128).astype(jnp.float32)
+        owner, rest = got[:, 0:1], got[:, 1:2]
+        onehot = jnp.where(owner == iota((some, 128), 1), 1.0, 0.0)
+        before = jnp.dot(lower, onehot.astype(jnp.bfloat16), preferred_element_type=jnp.float32)
+        return owner, rest, jnp.sum(before * onehot, axis=1, keepdims=True)
+
+    for n in range(quarter // batch):
+        owner, rest, earlier = decode(tp * quarter + n * batch)
+        slot = owner * (quarter * capacity) + (source + n * batch) * capacity + earlier
+        table[n * some : (n + 1) * some, :] = jnp.where(
+            slot == iota((some, table.shape[1]), 1), 1.0, 0.0
+        ).astype(jnp.bfloat16)
+    place[...] = jnp.zeros_like(place)
+
+    @pl.loop(0, groups // batch)
+    def _(n):
+        owner, rest, earlier = decode(n * batch)
+        here = (rest == iota((some, tokens), 1)) & (owner == rank.astype(jnp.float32))
+        slot = (source + (n * batch).astype(jnp.float32)) * capacity + earlier
+        there = slot == iota((some, 128), 1)
+        place[...] += lax.dot_general(
+            jnp.where(here, 1.0, 0.0).astype(jnp.bfloat16),
+            jnp.where(there, 1.0, 0.0).astype(jnp.bfloat16),
+            (((0,), (0,)), ((), ())),
+            preferred_element_type=jnp.float32,
+        )
+
+    for k in range(3):
+        pltpu.make_async_copy(landed.at[k], landed.at[k], y_recv.at[k]).wait()
+        mine = mine + landed[k].astype(jnp.float32)
+    packed[...] = lax.dot_general(
+        table[...],
+        mine.astype(jnp.bfloat16),
+        (((0,), (0,)), ((), ())),
         preferred_element_type=jnp.float32,
-    )
+    ).astype(jnp.bfloat16)
+
+    piece = quarter * capacity
+    to_tp = rank // 8
+    lane_group = rank % 8
+
+    def sending(i):
+        j = (rank + i) % groups
+        return remote(
+            packed.at[pl.ds(pl.multiple_of(j * piece, piece), piece)],
+            arrived.at[lane_group, pl.ds(pl.multiple_of(tp * piece, piece), piece)],
+            d_send.at[i],
+            d_recv.at[lane_group * 4 + tp],
+            j // 16,
+            j % 16,
+            to_tp,
+        )
+
+    def staying():
+        return pltpu.make_async_copy(
+            packed.at[pl.ds(pl.multiple_of(rank * piece, piece), piece)],
+            arrived.at[lane_group, pl.ds(pl.multiple_of(tp * piece, piece), piece)],
+            d_recv.at[lane_group * 4 + tp],
+        )
+
+    @pl.when(to_tp == tp)
+    def _():
+        staying().start()
+
+    @pl.when(to_tp != tp)
+    def _():
+        sending(0).start()
+
+    @pl.loop(1, groups)
+    def _(i):
+        sending(i).start()
+
+    chosen = place[...].astype(jnp.bfloat16)
+    hit = jnp.max(place[...], axis=1, keepdims=True) > 0.5
+    for c in range(8):
+        for k in range(4):
+            got = arrived.at[c, pl.ds(k * piece, piece)]
+            pltpu.make_async_copy(got, got, d_recv.at[c * 4 + k]).wait()
+        rows_here = jnp.dot(chosen, arrived[c], preferred_element_type=jnp.float32)
+        span = slice(c * columns, (c + 1) * columns)
+        stream[:, span] = jnp.where(
+            hit, rows_here, prompt[:, span].astype(jnp.float32)
+        ).astype(jnp.bfloat16)
+    for copy in copies:
+        copy.wait_send()
+
+    @pl.when(to_tp != tp)
+    def _():
+        sending(0).wait_send()
+
+    @pl.loop(1, groups)
+    def _(i):
+        sending(i).wait_send()
+
+
+def merge(hidden, weight, position, prompt):
+    rows, width = hidden.shape
+    groups = lax.axis_size("role") * lax.axis_size("seq")
+    columns = weight.shape[1]
+    block = groups * rows // 4
+    slots = groups * (groups // 4) * (2 * rows // groups)
+    dma = pltpu.SemaphoreType.DMA
+    vmem = pl.BlockSpec(memory_space=pltpu.VMEM)
+    return pl.pallas_call(
+        merge_kernel,
+        out_shape=jax.ShapeDtypeStruct(prompt.shape, jnp.bfloat16),
+        in_specs=[vmem] * 4,
+        out_specs=vmem,
+        scratch_shapes=[
+            pltpu.VMEM((groups, rows, width + 128), jnp.bfloat16),
+            dma((groups,)),
+            dma((groups, 2)),
+            dma((PLANE_SENDS,)),
+            pltpu.VMEM((3, block, columns), jnp.bfloat16),
+            pltpu.VMEM((3, block, columns), jnp.bfloat16),
+            dma((3,)),
+            dma((3,)),
+            pltpu.VMEM((block, slots), jnp.bfloat16),
+            pltpu.VMEM((prompt.shape[0], 128), jnp.float32),
+            pltpu.VMEM((slots, columns), jnp.bfloat16),
+            pltpu.VMEM((8, slots // 8, columns), jnp.bfloat16),
+            dma((groups,)),
+            dma((groups,)),
+        ],
+        compiler_params=pltpu.CompilerParams(
+            has_side_effects=True, vmem_limit_bytes=48 << 20
+        ),
+    )(hidden, weight, position[:, None], prompt)
 
 
 KEY_BLOCK = 1024
@@ -145,51 +394,11 @@
     key_weight,
     value_weight,
 ):
-    groups = lax.axis_size("role") * lax.axis_size("seq")
     device_rank = lax.axis_index(("role", "seq"))
-    row_count = merger_hidden.shape[0]
     tok_count = prompt_embeds.shape[0]
     columns = prompt_embeds.shape[1]
     model_width = columns * lax.axis_size("tp")
-    capacity = 2 * row_count // groups
-    strips = project_strips(merger_hidden, merger_out)
-    partial_value = lax.all_to_all(strips, ("role", "seq"), split_axis=0, concat_axis=1, tiled=True)
-    embeds = sum_hidden(partial_value)
-    owners = jnp.where(row_position >= 0, row_position // tok_count, groups)
-    onehot = (owners[:, None] == jnp.arange(groups, dtype=jnp.int32)[None, :]).astype(jnp.int32)
-    earlier = jnp.sum((jnp.cumsum(onehot, axis=0) - onehot) * onehot, axis=1)
-    buffer_slot = jnp.where(owners < groups, owners * capacity + earlier, groups * capacity)
-    source = (
-        jnp.full((groups * capacity,), row_count, jnp.int32)
-        .at[buffer_slot]
-        .set(jnp.arange(row_count, dtype=jnp.int32), mode="drop")
-    )
-    padded = jnp.concatenate([embeds, jnp.zeros((1, columns), jnp.bfloat16)], axis=0)
-    outgoing = padded[source].reshape(groups, capacity, columns)
-    outgoing_pos = jnp.concatenate([row_position, jnp.full((1,), -1, jnp.int32)])[source].reshape(
-        groups, capacity
-    )
-    role_count = lax.axis_size("role")
-    seq_count = lax.axis_size("seq")
-    arrived, arrived_pos = (
-        exchange_both(
-            outgoing.reshape(role_count, seq_count, capacity, columns),
-            ("role", "seq"),
-            ("role", "seq"),
-            (0, 1),
-            (0, 1),
-        ),
-        exchange_both(
-            outgoing_pos.reshape(role_count, seq_count, capacity),
-            ("role", "seq"),
-            ("role", "seq"),
-            (0, 1),
-            (0, 1),
-        ),
-    )
-    arrived_pos = arrived_pos.reshape(-1)
-    local_row = jnp.where(arrived_pos >= 0, arrived_pos - device_rank * tok_count, tok_count)
-    stream = prompt_embeds.at[local_row].set(arrived.reshape(-1, columns), mode="drop")
+    stream = merge(merger_hidden, merger_out, row_position, prompt_embeds)
     widened = stream.astype(jnp.float32)
     squares = lax.psum(jnp.sum(widened * widened, axis=1), "tp")
     inverse = lax.rsqrt(squares / model_width + 1e-06)[:, None]

time: 311 us -> 238 us (0.77)
  waiting for transfers between devices: 163 us -> 82.4 us
  Pallas kernels: 40 us -> 107 us
  blocking collectives: 39 us -> 6 us
  starting transfers between devices: 14 us -> 0.26 us
  local copies, waits for them, and re-layouts: 16.2 us -> 8.61 us
  matrix products: 18.4 us -> 14.3 us
    pallas_call x0 -> x1, Pallas kernels: none -> 66.7 us  [merge(): pl.pallas_call(merge_kernel, out_shape=jax.ShapeDtypeStruct(prompt.shape,...]
    all_gather x1 -> x0, waiting for transfers between devices: 51 us -> none  [project_strips(): lax.all_gather(merger_hidden, ('role', 'seq'), axis=0, tiled=True)]
    all_to_all x1 -> x0, blocking collectives: 32.4 us -> none  [body(): lax.all_to_all(strips, ('role', 'seq'), split_axis=0, concat_axis=1, tile...]
    reduce_scatter x1 -> x0, waiting for transfers between devices: 19.1 us -> none  [sum_hidden(): lax.psum_scatter(partial_value, 'tp', scatter_dimension=1, tiled=True)]
    all_to_all x2 -> x0, starting transfers between devices: 13.7 us -> none  [exchange_both(): lax.all_to_all(blocks, axis, split_axis=0, concat_axis=0, tiled=True)]
    all_to_all x2 -> x0, waiting for transfers between devices: 9.39 us -> none  [exchange_both(): lax.all_to_all(blocks, axis, split_axis=0, concat_axis=0, tiled=True)]
    another operation x3 -> x0, local copies, waits for them, and re-layouts: 4.78 us -> none  [the longest x2 2.83 us: exchange_both(): blocks = blocks.reshape(-1, *inside)]
    unnamed x18 -> x17, local copies, waits for them, and re-layouts: 0.96 us -> 5.31 us
  transfers between devices with their start and end apart: 6 -> 2, of which waited for: 5 -> 2; matrix products, arithmetic and copies ran while one was open for 6% -> 5% of each run, Pallas kernels for 0% -> 0%
where the time goes in v2:
time: 238 us
  Pallas kernels  107 us (45%)
  waiting for transfers between devices  82.4 us (35%)
  matrix products  14.3 us (6%)
  between operations  14.2 us (6%)
  local copies, waits for them, and re-layouts  8.61 us (4%)
  blocking collectives  6 us (3%)
  other arithmetic  5.11 us (2%)
    pallas_call x1, Pallas kernels, merge(): pl.pallas_call(merge_kernel, out_shape=jax.ShapeDtypeStruct(prompt.shape,...  66.7 us
    all_gather x1, waiting for transfers between devices, body(): shard_piece = lax.all_gather(normed, 'tp', axis=1, tiled=True)  47.6 us
    pallas_call x1, Pallas kernels, attend(): pl.pallas_call(functools.partial(attend_kernel, heads), out_shape=jax.Sha...  40 us
    all_gather x1, waiting for transfers between devices, sent_together(): filled = lax.all_gather(both, axis, axis=dim, tiled=True)  34.8 us
    dot_general x3, matrix products, body(): jnp.dot(shard_piece, table, preferred_element_type=jnp.float32)  14.3 us
    psum x1, blocking collectives, body(): squares = lax.psum(jnp.sum(widened * widened, axis=1), 'tp')  6 us
    unnamed x17, local copies, waits for them, and re-layouts  5.31 us
  transfers between devices with their start and end apart: 2, of which 2 were waited for; matrix products, arithmetic and copies ran while one was open for 5% of the time, Pallas kernels for 0%

profile of v2, /device:TPU:97, one launch (start us, length us, event | category | flops | bytes accessed | tf_op | source)
XLA Modules:
  0.0 237.7 jit_solution(17219999748800790474)
XLA Ops:
  7.2 0.8 convert_element_type.35
  8.1 0.7 copy.12.position
  8.8 1.2 copy-done.2
  10.0 1.1 copy-done.3
  11.1 0.9 copy-done.4
  12.0 66.7 %shard_map.95 = bf16[256,2048]{1,0:T(8,128)(2,1)S(1)} custom-call(bf16[64,1280]{1,0:T(8,128)(2,1)S(1)} %copy-done.4, bf16[1280,256]{1,0:T(8,128)(2,1)S(1)} %copy-done.3, s32[64,1]{1,0:T(8,128)S(1)} %copy.12.position, bf16[256,2048]{1,0:T(8,128)(2,1)S(1)} %copy-done.2), custom_call_target="tpu_custom_call" | custom-call | tf_op jit(solution)/shard_map/pallas_call | solution.py:296
  78.8 0.3 fusion
  79.1 6.0 %psum.7 = f32[256]{0:T(256)S(1)} all-reduce(f32[256]{0:T(256)S(1)} %fusion), channel_id=1, replica_groups=mesh['role'=2,'seq'=16,'tp'=4] {'tp'}, use_global_device_ids=true, to_apply=%region_1.0 | all-reduce | flops 256 | bytes 2048 | tf_op jit(solution)/shard_map/psum | solution.py:403
  85.1 1.3 fusion.2
  86.4 0.2 all-gather.5.cloned.1.call-start
  86.6 47.6 %all-gather.3.cloned.1.call-done = bf16[256,8192]{1,0:T(8,128)(2,1)} async-done(((bf16[256,2048]{1,0:T(8,128)(2,1)}), bf16[256,8192]{1,0:T(8,128)(2,1)}) %all-gather.3.cloned.1.call-update) | async-done | bytes 4194320 | tf_op jit(solution)/shard_map/all_gather | solution.py:407
  134.2 3.6 %convolution_bitcast_fusion.1 = f32[256,1,128]{2,0,1:T(8,128)S(1)} fusion(bf16[256,8192]{1,0:T(8,128)(2,1)} %all-gather.3.cloned.1.call-done, bf16[8192,128]{1,0:T(8,128)(2,1)S(1)} %copy-done), kind=kOutput, calls=%fused_computation.8 | convolution fusion | flops 536870912 | bytes 6422528 | tf_op jit(solution)/shard_map/dot_general | solution.py:409
  137.9 0.6 fusion.9
  138.5 1.2 fusion.3
  139.7 0.7 pad_maximum_fusion.1
  140.5 0.5 multiply_cosine_fusion.1
  141.0 9.4 %convolution_bitcast_fusion = f32[32,8,8,128]{3,1,2,0:T(8,128)S(1)} fusion(bf16[256,8192]{1,0:T(8,128)(2,1)} %all-gather.3.cloned.1.call-done, bf16[8192,1024]{1,0:T(8,128)(2,1)} %param.13), kind=kOutput, calls=%fused_computation.7 | convolution fusion | flops 4294967296 | bytes 22020096 | tf_op jit(solution)/shard_map/dot_general | solution.py:409
  150.7 0.5 subtract_convert_fusion
  151.2 0.3 pad_maximum_fusion
  151.5 0.9 copy.19
  152.4 34.8 %all-gather.5.cloned.1.call-done = bf16[8192,2,128]{2,0,1:T(8,128)(2,1)} async-done(((bf16[256,2,128]{2,0,1:T(8,128)(2,1)}), bf16[8192,2,128]{2,0,1:T(8,128)(2,1)}) %all-gather.5.cloned.1.call-update) | async-done | bytes 4194320 | tf_op jit(solution)/shard_map/all_gather | solution.py:17
  187.2 2.6 %slice_bitcast_fusion = (bf16[8192,128]{1,0:T(8,128)(2,1)S(1)}, bf16[8192,128]{1,0:T(8,128)(2,1)S(1)}) fusion(bf16[8192,2,128]{2,0,1:T(8,128)(2,1)} %all-gather.5.cloned.1.call-done), kind=kLoop, calls=%fused_computation.5 | loop fusion | bytes 8388608 | tf_op jit(solution)/shard_map/reshape | solution.py:425
  189.8 40.0 %shard_map.96 = bf16[256,1024]{1,0:T(8,128)(2,1)} custom-call(bf16[256,1024]{1,0:T(8,128)(2,1)S(1)} %bitcast.22, bf16[8192,128]{1,0:T(8,128)(2,1)S(1)} %get-tuple-element.3.k_ref, bf16[8192,128]{1,0:T(8,128)(2,1)S(1)} %get-tuple-element.2.v_ref), custom_call_target="tpu_custom_call" | custom-call | tf_op jit(solution)/shard_map/pallas_call | solution.py:377
  229.8 1.0 copy.21
  (18 shorter events, 0.3 us)
Async XLA Ops:
  7.2 127.1 %copy-start = (bf16[8192,128]{1,0:T(8,128)(2,1)S(1)}, bf16[8192,128]{1,0:T(8,128)(2,1)}, u32[]{:S(2)}) copy-start(bf16[8192,128]{1,0:T(8,128)(2,1)} %param.14) | copy-start | bytes 6291460
  7.2 127.0 %all-gather.3.cloned.1.call-start = ((), (), s32[]{:S(2)}) async-start(), calls=%async_computation | async-start | bytes 5242880 | tf_op jit(solution)/shard_map/all_gather | solution.py:407
  8.8 1.2 copy-start.2
  10.0 1.1 copy-start.3
  11.1 0.9 copy-start.4
  86.4 100.9 %all-gather.5.cloned.1.call-start = ((), (), s32[]{:S(2)}) async-start(), calls=%async_computation.1 | async-start | bytes 4325376 | tf_op jit(solution)/shard_map/all_gather | solution.py:17
  134.2 4.2 %copy-start.5 = (bf16[256,8192]{1,0:T(8,128)(2,1)S(1)}, bf16[256,8192]{1,0:T(8,128)(2,1)}, u32[]{:S(2)}) copy-start(bf16[256,8192]{1,0:T(8,128)(2,1)} %all-gather.3.cloned.1.call-done) | copy-start | bytes 12582916
  134.2 4.2 %copy-start.6 = (bf16[8192,128]{1,0:T(8,128)(2,1)S(1)}, bf16[8192,128]{1,0:T(8,128)(2,1)}, u32[]{:S(2)}) copy-start(bf16[8192,128]{1,0:T(8,128)(2,1)} %param.15) | copy-start | bytes 6291460
  187.2 2.6 %copy-start.1 = (bf16[32,8,8,128]{3,1,2,0:T(8,128)(2,1)S(1)}, bf16[32,8,8,128]{3,1,2,0:T(8,128)(2,1)}, u32[]{:S(2)}) copy-start(bf16[32,8,8,128]{3,1,2,0:T(8,128)(2,1)} %copy.19) | copy-start | bytes 1572868
Sparse Core Ops, SparseCore 0:
  86.5 47.6 all-gather.2
  140.6 46.5 all-gather.4

commit v3 on v2

--- a/solution.py
+++ b/solution.py
@@ -11,27 +11,14 @@
 HEAD_DIM = 128
 
 
-def sent_together(arrays, axis, dim, along):
-    widths = [a.shape[along] for a in arrays]
-    both = jnp.concatenate(arrays, axis=along)
-    filled = lax.all_gather(both, axis, axis=dim, tiled=True)
-    return tuple(jnp.split(filled, [sum(widths[:k]) for k in range(1, len(widths))], axis=along))
-
-
-def rotate(vectors, positions):
-    half_dim = vectors.shape[-1] // 2
+def rotary(positions):
+    half_dim = HEAD_DIM // 2
     frequency = 1000000.0 ** (-jnp.arange(half_dim, dtype=jnp.float32) / half_dim)
-    angles = positions.astype(jnp.float32)[:, None, None] * frequency[None, None, :]
-    cosine = jnp.cos(angles)
-    sine_part = jnp.sin(angles)
-    lower_half = vectors[..., :half_dim]
-    upper_half = vectors[..., half_dim:]
-    return jnp.concatenate(
-        [
-            lower_half * cosine - upper_half * sine_part,
-            upper_half * cosine + lower_half * sine_part,
-        ],
-        axis=-1,
+    angles = positions.astype(jnp.float32)[:, None] * frequency[None, :]
+    cosine, sine = jnp.cos(angles), jnp.sin(angles)
+    return (
+        jnp.concatenate([cosine, cosine], axis=1),
+        jnp.concatenate([-sine, sine], axis=1),
     )
 
 
@@ -320,23 +307,205 @@
     )(hidden, weight, position[:, None], prompt)
 
 
+CHUNKS = 4
+
+
+def project_kernel(
+    eps,
+    stream,
+    gain,
+    query_weight,
+    key_weight,
+    value_weight,
+    cosine,
+    sine,
+    queries,
+    both,
+    normed,
+    weights,
+    acc,
+    squares,
+    w_sem,
+    s_send,
+    s_recv,
+    n_send,
+    n_recv,
+):
+    role, seq, tp = lax.axis_index("role"), lax.axis_index("seq"), lax.axis_index("tp")
+    rows, columns = stream.shape
+    chunk = columns // CHUNKS
+    heads = queries.shape[1] // HEAD_DIM
+    parts = ((query_weight, 0), (key_weight, heads), (value_weight, heads + 1))
+    fetches = {}
+    for i, off in enumerate((0, -1, 1, 2)):
+        t = (tp + off + 4) % 4
+        for k, (table, place) in enumerate(parts):
+            span = pl.ds(pl.multiple_of(t * columns, columns), columns)
+            lanes = pl.ds(place * HEAD_DIM, table.shape[1])
+            copy = pltpu.make_async_copy(
+                table.at[span], weights.at[span, lanes], w_sem.at[i, k]
+            )
+            copy.start()
+            fetches[off, k] = copy
+
+    total = jnp.zeros((rows, 128), jnp.float32)
+    for c in range(columns // 128):
+        x = stream[:, c * 128 : (c + 1) * 128].astype(jnp.float32)
+        total = total + x * x
+    squares[3] = jnp.broadcast_to(
+        jnp.sum(jnp.transpose(total), axis=0, keepdims=True), (8, rows)
+    )
+    sums = []
+    for k, off in enumerate((1, 3, 2)):
+        copy = remote(
+            squares.at[3], squares.at[k], s_send.at[k], s_recv.at[k], role, seq, (tp + off) % 4
+        )
+        copy.start()
+        sums.append(copy)
+    for copy in sums:
+        copy.wait()
+    whole = squares[0] + squares[1] + (squares[2] + squares[3])
+    whole = jnp.broadcast_to(whole[0:1], (128, rows))
+    inverse = lax.rsqrt(jnp.transpose(whole) / (4 * columns) + eps)[:, 0:1]
+
+    copies = []
+
+    def send(t, c, off):
+        copy = remote(
+            normed.at[t, c],
+            normed.at[t, c],
+            n_send.at[len(copies)],
+            n_recv.at[t, c],
+            role,
+            seq,
+            (tp + off + 4) % 4,
+        )
+        copy.start()
+        copies.append(copy)
+
+    def arrive(t, c):
+        pltpu.make_async_copy(normed.at[t, c], normed.at[t, c], n_recv.at[t, c]).wait()
+
+    def scale(c):
+        span = slice(c * chunk, (c + 1) * chunk)
+        x = stream[:, span].astype(jnp.float32)
+        normed[tp, c] = (x * inverse * gain[:, span].astype(jnp.float32)).astype(jnp.bfloat16)
+
+    scale(0)
+    send(tp, 0, 1)
+    scale(2)
+    send(tp, 2, -1)
+    scale(1)
+    send(tp, 1, 1)
+    scale(3)
+    send(tp, 3, -1)
+    send(tp, 2, 1)
+    send(tp, 0, -1)
+    send(tp, 3, 1)
+    send(tp, 1, -1)
+    before, after, across = (tp + 3) % 4, (tp + 1) % 4, (tp + 2) % 4
+
+    def multiply(t, c, first=False):
+        span = pl.ds(pl.multiple_of(t * columns + c * chunk, chunk), chunk)
+        value = jnp.dot(normed[t, c], weights[span, :], preferred_element_type=jnp.float32)
+        if first:
+            acc[...] = value
+        else:
+            acc[...] += value
+
+    def fetched(off):
+        for k in range(len(parts)):
+            fetches[off, k].wait()
+
+    fetched(0)
+    for c in range(CHUNKS):
+        multiply(tp, c, c == 0)
+    fetched(-1)
+    fetched(1)
+    for c, d in ((0, 2), (1, 3)):
+        arrive(before, c)
+        send(before, c, 1)
+        arrive(after, d)
+        send(after, d, -1)
+        multiply(before, c)
+        multiply(after, d)
+    for c, d in ((2, 0), (3, 1)):
+        arrive(before, c)
+        multiply(before, c)
+        arrive(after, d)
+        multiply(after, d)
+    fetched(2)
+    for c in (0, 2, 1, 3):
+        arrive(across, c)
+        multiply(across, c)
+
+    for h in range(heads + 1):
+        span = slice(h * HEAD_DIM, (h + 1) * HEAD_DIM)
+        u = acc[:, span]
+        turned = u * cosine[...] + pltpu.roll(u, HEAD_DIM // 2, 1) * sine[...]
+        if h < heads:
+            queries[:, span] = turned.astype(jnp.bfloat16)
+        else:
+            both[:, :HEAD_DIM] = turned.astype(jnp.bfloat16)
+    both[:, HEAD_DIM:] = acc[:, (heads + 1) * HEAD_DIM :].astype(jnp.bfloat16)
+    for copy in copies:
+        copy.wait_send()
+
+
+def project(stream, gain, query_weight, key_weight, value_weight, cosine, sine):
+    rows, columns = stream.shape
+    wide = query_weight.shape[1] + 2 * HEAD_DIM
+    dma = pltpu.SemaphoreType.DMA
+    vmem = pl.BlockSpec(memory_space=pltpu.VMEM)
+    hbm = pl.BlockSpec(memory_space=pl.ANY)
+    return pl.pallas_call(
+        functools.partial(project_kernel, 1e-06),
+        out_shape=(
+            jax.ShapeDtypeStruct((rows, query_weight.shape[1]), jnp.bfloat16),
+            jax.ShapeDtypeStruct((rows, 2 * HEAD_DIM), jnp.bfloat16),
+        ),
+        in_specs=[vmem, vmem, hbm, hbm, hbm, vmem, vmem],
+        out_specs=(vmem, vmem),
+        scratch_shapes=[
+            pltpu.VMEM((4, CHUNKS, rows, columns // CHUNKS), jnp.bfloat16),
+            pltpu.VMEM((4 * columns, wide), jnp.bfloat16),
+            pltpu.VMEM((rows, wide), jnp.float32),
+            pltpu.VMEM((4, 8, rows), jnp.float32),
+            dma((4, 3)),
+            dma((3,)),
+            dma((3,)),
+            dma((3 * CHUNKS,)),
+            dma((4, CHUNKS)),
+        ],
+        compiler_params=pltpu.CompilerParams(
+            has_side_effects=True, vmem_limit_bytes=56 << 20
+        ),
+    )(stream, gain, query_weight, key_weight, value_weight, cosine, sine)
+
+
 KEY_BLOCK = 1024
 
 
-def attend_kernel(heads, q_ref, k_ref, v_ref, o_ref, acc, top, total):
+def attend_kernel(
+    heads, q_ref, both, o_ref, buf, full_sem, half_sem, send_sem, acc, top, total
+):
     rows = q_ref.shape[0]
-    first = (lax.axis_index("role") * lax.axis_size("seq") + lax.axis_index("seq")) * rows
+    rank = lax.axis_index("role") * lax.axis_size("seq") + lax.axis_index("seq")
+    first = rank * rows
+    several = KEY_BLOCK // rows
     factor = math.log2(math.e) / math.sqrt(HEAD_DIM)
+    buf[rank] = both[...]
+    plane_gather(buf, full_sem, half_sem, send_sem)
     acc[...] = jnp.zeros_like(acc)
     total[...] = jnp.zeros_like(total)
     top[...] = jnp.full_like(top, -1e30)
 
     def block(b, masked):
-        start = pl.multiple_of(b * KEY_BLOCK, KEY_BLOCK)
-        k = k_ref[pl.ds(start, KEY_BLOCK), :]
-        v = v_ref[pl.ds(start, KEY_BLOCK), :]
+        got = pl.ds(b * several, several)
+        k = buf[got, :, :HEAD_DIM].reshape(KEY_BLOCK, HEAD_DIM)
+        v = buf[got, :, HEAD_DIM:].reshape(KEY_BLOCK, HEAD_DIM)
         if masked:
-            key_pos = start + lax.broadcasted_iota(jnp.int32, (rows, KEY_BLOCK), 1)
+            key_pos = b * KEY_BLOCK + lax.broadcasted_iota(jnp.int32, (rows, KEY_BLOCK), 1)
             query_pos = first + lax.broadcasted_iota(jnp.int32, (rows, KEY_BLOCK), 0)
             visible = key_pos <= query_pos
         for h in range(heads):
@@ -371,17 +540,28 @@
         o_ref[:, h * HEAD_DIM : (h + 1) * HEAD_DIM] = (acc[h] / l).astype(o_ref.dtype)
 
 
-def attend(q, k, v, heads):
+def attend(q, both):
     rows = q.shape[0]
+    heads = q.shape[1] // HEAD_DIM
+    groups = lax.axis_size("role") * lax.axis_size("seq")
+    dma = pltpu.SemaphoreType.DMA
     vmem = pl.BlockSpec(memory_space=pltpu.VMEM)
     return pl.pallas_call(
         functools.partial(attend_kernel, heads),
         out_shape=jax.ShapeDtypeStruct(q.shape, jnp.bfloat16),
-        in_specs=[vmem] * 3,
+        in_specs=[vmem] * 2,
         out_specs=vmem,
-        scratch_shapes=[pltpu.VMEM((heads, rows, HEAD_DIM), jnp.float32)] * 3,
-        compiler_params=pltpu.CompilerParams(vmem_limit_bytes=48 << 20),
-    )(q, k, v)
+        scratch_shapes=[
+            pltpu.VMEM((groups, rows, 2 * HEAD_DIM), jnp.bfloat16),
+            dma((groups,)),
+            dma((groups, 2)),
+            dma((PLANE_SENDS,)),
+        ]
+        + [pltpu.VMEM((heads, rows, HEAD_DIM), jnp.float32)] * 3,
+        compiler_params=pltpu.CompilerParams(
+            has_side_effects=True, vmem_limit_bytes=48 << 20
+        ),
+    )(q, both)
 
 
 def body(
@@ -396,35 +576,13 @@
 ):
     device_rank = lax.axis_index(("role", "seq"))
     tok_count = prompt_embeds.shape[0]
-    columns = prompt_embeds.shape[1]
-    model_width = columns * lax.axis_size("tp")
     stream = merge(merger_hidden, merger_out, row_position, prompt_embeds)
-    widened = stream.astype(jnp.float32)
-    squares = lax.psum(jnp.sum(widened * widened, axis=1), "tp")
-    inverse = lax.rsqrt(squares / model_width + 1e-06)[:, None]
-    normed = (widened * inverse * norm_gain.astype(jnp.float32)[None, :]).astype(jnp.bfloat16)
-    tables = (query_weight, key_weight, value_weight)
-    shard_piece = lax.all_gather(normed, "tp", axis=1, tiled=True)
-    query_sum, key_sum, value_sum = tuple(
-        (jnp.dot(shard_piece, table, preferred_element_type=jnp.float32) for table in tables)
+    positions = device_rank * tok_count + jnp.arange(tok_count, dtype=jnp.int32)
+    cosine, sine = rotary(positions)
+    queries, both = project(
+        stream, norm_gain[None, :], query_weight, key_weight, value_weight, cosine, sine
     )
-    local_heads = query_weight.shape[1] // HEAD_DIM
-    local_kv = key_weight.shape[1] // HEAD_DIM
-    positions = device_rank * tok_count + jnp.arange(tok_count, dtype=jnp.int32)
-    queries = rotate(query_sum.reshape(tok_count, local_heads, HEAD_DIM), positions).astype(
-        jnp.bfloat16
-    )
-    key_rows = rotate(key_sum.reshape(tok_count, local_kv, HEAD_DIM), positions).astype(
-        jnp.bfloat16
-    )
-    value_rows = value_sum.astype(jnp.bfloat16).reshape(tok_count, local_kv, HEAD_DIM)
-    key_piece, value_piece = sent_together((key_rows, value_rows), ("role", "seq"), 0, 1)
-    context = attend(
-        queries.reshape(tok_count, local_heads * HEAD_DIM),
-        key_piece.reshape(-1, HEAD_DIM),
-        value_piece.reshape(-1, HEAD_DIM),
-        local_heads,
-    )
+    context = attend(queries, both)
     return (stream, context)
 
 

time: 238 us -> 195 us (0.82)
  waiting for transfers between devices: 82.4 us -> 0 us
  Pallas kernels: 107 us -> 183 us
  matrix products: 14.3 us -> 0 us
  between operations: 14.2 us -> 0.72 us
  blocking collectives: 6 us -> 0 us
  other arithmetic: 5.11 us -> 1.38 us
    all_gather x2 -> x0, waiting for transfers between devices: 82.4 us -> none  [the longest x1 47.6 us: body(): shard_piece = lax.all_gather(normed, 'tp', axis=1, tiled=True)]
    pallas_call x0 -> x1, Pallas kernels: none -> 47.2 us  [project(): pl.pallas_call(functools.partial(project_kernel, 1e-06), out_shape=(jax.S...]
    pallas_call x1, Pallas kernels: 40 us -> 69.5 us  [attend(): pl.pallas_call(functools.partial(attend_kernel, heads), out_shape=jax.Sha...]
    dot_general x3 -> x0, matrix products: 14.3 us -> none  [body(): jnp.dot(shard_piece, table, preferred_element_type=jnp.float32)]
    psum x1 -> x0, blocking collectives: 6 us -> none  [body(): squares = lax.psum(jnp.sum(widened * widened, axis=1), 'tp')]
    unnamed x17 -> x18, local copies, waits for them, and re-layouts: 5.31 us -> 7.9 us
    reshape x1 -> x0, local copies, waits for them, and re-layouts: 2.55 us -> none  [body(): value_piece.reshape(-1, HEAD_DIM)]
  transfers between devices with their start and end apart: 2 -> 0, of which waited for: 2 -> 0; matrix products, arithmetic and copies ran while one was open for 5% -> 0% of each run, Pallas kernels for 0% -> 0%
where the time goes in v3:
time: 195 us
  Pallas kernels  183 us (94%)
  local copies, waits for them, and re-layouts  9.25 us (5%)
    pallas_call x1, Pallas kernels, attend(): pl.pallas_call(functools.partial(attend_kernel, heads), out_shape=jax.Sha...  69.5 us
    pallas_call x1, Pallas kernels, merge(): pl.pallas_call(merge_kernel, out_shape=jax.ShapeDtypeStruct(prompt.shape,...  66.7 us
    pallas_call x1, Pallas kernels, project(): pl.pallas_call(functools.partial(project_kernel, 1e-06), out_shape=(jax.S...  47.2 us
    unnamed x18, local copies, waits for them, and re-layouts  7.9 us

profile of v3, /device:TPU:97, one launch (start us, length us, event | category | flops | bytes accessed | tf_op | source)
XLA Modules:
  0.0 194.8 jit_solution(2641414670854398565)
XLA Ops:
  0.6 0.0 copy-start.7
  0.7 0.5 fusion
  1.2 0.8 pad_maximum_fusion
  2.0 0.7 copy.10.position
  2.8 0.0 copy-start.2
  2.8 1.2 copy-done.2
  4.0 0.0 copy-start.3
  4.0 1.1 copy-done.3
  5.1 0.0 copy-start.5
  5.1 0.9 copy-done.5
  6.0 66.7 %shard_map.95.stream = bf16[256,2048]{1,0:T(8,128)(2,1)S(1)} custom-call(bf16[64,1280]{1,0:T(8,128)(2,1)S(1)} %copy-done.5, bf16[1280,256]{1,0:T(8,128)(2,1)S(1)} %copy-done.3, s32[64,1]{1,0:T(8,128)S(1)} %copy.10.position, bf16[256,2048]{1,0:T(8,128)(2,1)S(1)} %copy-done.2), custom_call_target="tpu_custom_call" | custom-call | tf_op jit(solution)/shard_map/pallas_call | solution.py:283
  72.7 0.0 copy-start
  72.8 1.0 copy-done
  73.7 0.0 copy-done.7
  73.7 0.6 broadcast_in_dim.9.gain
  74.3 0.0 copy-start.1
  74.3 47.2 %shard_map.96 = (bf16[256,1024]{1,0:T(8,128)(2,1)}, bf16[256,256]{1,0:T(8,128)(2,1)}) custom-call(bf16[256,2048]{1,0:T(8,128)(2,1)} %copy-done, bf16[1,2048]{1,0:T(2,128)(2,1)} %broadcast_in_dim.9.gain, bf16[8192,1024]{1,0:T(8,128)(2,1)} %query_weight.1, bf16[8192,128]{1,0:T(8,128)(2,1)} %key_weight.1, bf16[8192,128]{1,0:T(8,128)(2,1)} %value_weight.1, ...), custom_call_target="tpu_custom_call" | custom-call | tf_op jit(solution)/shard_map/pallas_call | solution.py:461
  121.6 0.0 copy-start.4
  121.6 1.0 copy-done.4
  122.6 0.9 copy-done.6
  123.5 69.5 %shard_map.97 = bf16[256,1024]{1,0:T(8,128)(2,1)S(1)} custom-call(bf16[256,1024]{1,0:T(8,128)(2,1)S(1)} %copy-done.4, bf16[256,256]{1,0:T(8,128)(2,1)S(1)} %copy-done.6), custom_call_target="tpu_custom_call" | custom-call | tf_op jit(solution)/shard_map/pallas_call | solution.py:549
  193.0 0.0 copy-done.1
  193.0 1.0 copy.13
  194.0 0.8 copy.14
  (3 shorter events, 0.0 us)
Async XLA Ops:
  0.6 73.1 %copy-start.7 = (bf16[2048]{0:T(1024)(128)(2,1)S(1)}, bf16[2048]{0:T(1024)(128)(2,1)}, u32[]{:S(2)}) copy-start(bf16[2048]{0:T(1024)(128)(2,1)} %param.12) | copy-start | bytes 12292
  2.8 1.2 copy-start.2
  4.0 1.1 copy-start.3
  5.1 0.9 copy-start.5
  72.7 1.0 copy-start
  74.3 118.7 %copy-start.1 = (bf16[256,2048]{1,0:T(8,128)(2,1)S(1)}, bf16[256,2048]{1,0:T(8,128)(2,1)}, u32[]{:S(2)}) copy-start(bf16[256,2048]{1,0:T(8,128)(2,1)} %copy-done) | copy-start | bytes 3145732
  121.6 1.0 copy-start.4
  122.6 0.9 copy-start.6

commit v4 on v3

v4 whole, which is shorter than its diff:
```python
import functools
import math

import jax
import jax.numpy as jnp
from jax import lax
from jax.experimental import pallas as pl
from jax.experimental.pallas import tpu as pltpu
from jax.sharding import PartitionSpec as P

HEAD_DIM = 128


def rotary(positions):
    half_dim = HEAD_DIM // 2
    frequency = 1000000.0 ** (-jnp.arange(half_dim, dtype=jnp.float32) / half_dim)
    angles = positions.astype(jnp.float32)[:, None] * frequency[None, :]
    cosine, sine = jnp.cos(angles), jnp.sin(angles)
    return (
        jnp.concatenate([cosine, cosine], axis=1),
        jnp.concatenate([-sine, sine], axis=1),
    )


MESH = pl.DeviceIdType.MESH
SIDE = 4


def remote(src, dst, send_sem, recv_sem, role, seq, tp):
    return pltpu.make_async_remote_copy(
        src_ref=src,
        dst_ref=dst,
        send_sem=send_sem,
        recv_sem=recv_sem,
        device_id=(role, seq, tp),
        device_id_type=MESH,
    )


def plane_gather(buf, full_sem, half_sem, send_sem, on_line=None):
    role, seq, tp = lax.axis_index("role"), lax.axis_index("seq"), lax.axis_index("tp")
    step_a, step_b = 1 + 3 * role, 4 - 3 * role
    z, x = seq // SIDE, seq % SIDE
    ca = x + role * (z - x)
    cb = z + role * (x - z)
    half = buf.shape[1] // 2
    sent = []

    def seq_of(a, b):
        return ((ca + a + SIDE) % SIDE) * step_a + ((cb + b + SIDE) % SIDE) * step_b

    def slot_of(a, b):
        return role * (SIDE * SIDE) + seq_of(a, b)

    def whole(slot, to_role, to_seq):
        copy = remote(
            buf.at[slot], buf.at[slot], send_sem.at[len(sent)], full_sem.at[slot], to_role, to_seq, tp
        )
        copy.start()
        sent.append(copy)

    def part(slot, k, to_seq):
        piece = buf.at[slot, pl.ds(k * half, half)]
        copy = remote(
            piece, piece, send_sem.at[len(sent)], half_sem.at[slot, k], role, to_seq, tp
        )
        copy.start()
        sent.append(copy)

    def wait_whole(slot):
        pltpu.make_async_copy(buf.at[slot], buf.at[slot], full_sem.at[slot]).wait()

    def wait_parts(slot):
        for k in range(2):
            piece = buf.at[slot, pl.ds(k * half, half)]
            pltpu.make_async_copy(piece, piece, half_sem.at[slot, k]).wait()

    def spread_b(slot):
        whole(slot, role, seq_of(0, 1))
        whole(slot, role, seq_of(0, -1))
        whole(slot, 1 - role, seq)

    own = slot_of(0, 0)
    whole(own, role, seq_of(1, 0))
    whole(own, role, seq_of(-1, 0))
    spread_b(own)
    for a, k in ((-1, 0), (1, 1)):
        wait_whole(slot_of(a, 0))
        part(slot_of(a, 0), k, seq_of(-a, 0))
        spread_b(slot_of(a, 0))

    def pass_b(a):
        for b, k in ((-1, 0), (1, 1)):
            wait_whole(slot_of(a, b))
            part(slot_of(a, b), k, seq_of(0, -b))
            whole(slot_of(a, b), 1 - role, seq)

    def line(b):
        if on_line is not None:
            on_line(role, (cb + b + SIDE) % SIDE)

    def other_line(b):
        fixed = (ca + b + SIDE) % SIDE
        for k in range(SIDE):
            wait_whole((1 - role) * (SIDE * SIDE) + fixed * step_a + k * step_b)
        if on_line is not None:
            on_line(1 - role, fixed)

    pass_b(0)
    wait_parts(slot_of(2, 0))
    spread_b(slot_of(2, 0))
    line(0)
    for a in (-1, 1):
        pass_b(a)
    other_line(0)
    pass_b(2)
    line(-1)
    line(1)
    other_line(-1)
    other_line(1)
    for a in (0, -1, 1, 2):
        wait_parts(slot_of(a, 2))
        whole(slot_of(a, 2), 1 - role, seq)
    line(2)
    other_line(2)
    return sent


PLANE_SENDS = 2 + 3 * 4 + 2 + 8 + 12
CHUNKS = 4
KEY_BLOCK = 1024


def iota(shape, dim):
    return lax.broadcasted_iota(jnp.int32, shape, dim).astype(jnp.float32)


def greet():
    role, seq, tp = lax.axis_index("role"), lax.axis_index("seq"), lax.axis_index("tp")
    z, x = seq // SIDE, seq % SIDE
    rank = role * (SIDE * SIDE) + seq
    barrier = pltpu.get_barrier_semaphore()

    def tell(to_role, to_seq, to_tp):
        pl.semaphore_signal(
            barrier, inc=1, device_id=(to_role, to_seq, to_tp), device_id_type=MESH
        )

    tell(1 - role, seq, tp)
    for k in (1, 3):
        tell(role, z * SIDE + (x + k) % SIDE, tp)
        tell(role, ((z + k) % SIDE) * SIDE + x, tp)
    for k in (1, 2, 3):
        tell(role, seq, (tp + k) % 4)

    @pl.loop(0, 32)
    def _(i):
        source = tp * 8 + i // 4

        @pl.when((source != rank) | (i % 4 != tp))
        def _():
            tell(source // 16, source % 16, i % 4)

    self_too = jnp.where(rank // 8 == tp, 1, 0)
    pl.semaphore_wait(barrier, 40 - self_too)


def merge_part(
    hidden, weight, position, prompt, stream, weight_here, prompt_here, m
):
    (
        buf,
        full_sem,
        half_sem,
        send_sem,
        partial,
        landed,
        mine,
        y_send,
        y_recv,
        table,
        place,
        packed,
        arrived,
        d_send,
        d_recv,
    ) = m
    role, seq, tp = lax.axis_index("role"), lax.axis_index("seq"), lax.axis_index("tp")
    rank = role * lax.axis_size("seq") + seq
    rows, width = hidden.shape
    tokens = prompt.shape[0]
    groups = buf.shape[0]
    columns = weight.shape[1]
    capacity = 2 * rows // groups
    quarter = groups // 4
    some = SIDE * rows
    copies = []

    def on_line(of_role, fixed):
        n = len(copies) // 3
        if n == 0:
            weight_here.wait()
        step_a, step_b = 1 + 3 * of_role, 4 - 3 * of_role
        pieces, spots = [], []
        for d in (2, 1, 3, 0):
            along = (tp + d + SIDE - fixed) % SIDE
            slot = of_role * (SIDE * SIDE) + along * step_a + fixed * step_b
            pieces.append(buf[slot, :, :width])
            spots.append(of_role * SIDE + fixed + of_role * (along - fixed))
        value = jnp.dot(
            jnp.concatenate(pieces, axis=0), weight[...], preferred_element_type=jnp.float32
        )
        for k, d in enumerate((2, 1, 3)):
            partial[n, k] = value[k * rows : (k + 1) * rows].astype(jnp.bfloat16)
            copy = remote(
                partial.at[n, k],
                landed.at[3 - d, spots[k]],
                y_send.at[n, k],
                y_recv.at[3 - d, spots[k]],
                role,
                seq,
                (tp + d) % 4,
            )
            copy.start()
            copies.append(copy)
        mine[spots[3]] = value[3 * rows :]

    sent = plane_gather(buf, full_sem, half_sem, send_sem, on_line)

    r0 = lax.broadcasted_iota(jnp.int32, (some, some), 0)
    r1 = lax.broadcasted_iota(jnp.int32, (some, some), 1)
    lower = jnp.where((r1 < r0) & (r1 // rows == r0 // rows), 1.0, 0.0).astype(jnp.bfloat16)
    source = lax.broadcasted_iota(jnp.int32, (some, 1), 0) // rows

    def decode(got):
        got = got.astype(jnp.float32)
        owner, rest = got[:, 0:1], got[:, 1:2]
        onehot = jnp.where(owner == iota((some, 128), 1), 1.0, 0.0)
        before = jnp.dot(lower, onehot.astype(jnp.bfloat16), preferred_element_type=jnp.float32)
        return owner, rest, jnp.sum(before * onehot, axis=1, keepdims=True)

    for n in range(quarter // SIDE):
        got = jnp.concatenate(
            [buf[n * 16 + z * SIDE + (tp + SIDE - z) % SIDE, :, width:] for z in range(SIDE)],
            axis=0,
        )
        owner, rest, earlier = decode(got)
        spot = (source + n * SIDE).astype(jnp.float32)
        slot = owner * (quarter * capacity) + spot * capacity + earlier
        table[n * some : (n + 1) * some, :] = jnp.where(
            slot == iota((some, table.shape[1]), 1), 1.0, 0.0
        ).astype(jnp.bfloat16)
    place[...] = jnp.zeros_like(place)

    @pl.loop(0, groups // SIDE)
    def _(n):
        got = buf[pl.ds(n * SIDE, SIDE), :, width:].reshape(some, 128)
        owner, rest, earlier = decode(got)
        here = (rest == iota((some, tokens), 1)) & (owner == rank.astype(jnp.float32))
        spot = ((source + n % SIDE) % SIDE) * quarter + n
        slot = spot.astype(jnp.float32) * capacity + earlier
        there = slot == iota((some, 128), 1)
        place[...] += lax.dot_general(
            jnp.where(here, 1.0, 0.0).astype(jnp.bfloat16),
            jnp.where(there, 1.0, 0.0).astype(jnp.bfloat16),
            (((0,), (0,)), ((), ())),
            preferred_element_type=jnp.float32,
        )

    for i in range(quarter):
        for k in range(3):
            got = landed.at[k, i]
            pltpu.make_async_copy(got, got, y_recv.at[k, i]).wait()
            mine[i] += landed[k, i].astype(jnp.float32)
    packed[...] = lax.dot_general(
        table[...],
        mine[...].reshape(quarter * rows, columns).astype(jnp.bfloat16),
        (((0,), (0,)), ((), ())),
        preferred_element_type=jnp.float32,
    ).astype(jnp.bfloat16)

    piece = quarter * capacity
    to_tp = rank // 8
    lane_group = rank % 8

    def sending(i):
        j = (rank + i) % groups
        return remote(
            packed.at[pl.ds(pl.multiple_of(j * piece, piece), piece)],
            arrived.at[lane_group, pl.ds(pl.multiple_of(tp * piece, piece), piece)],
            d_send.at[i],
            d_recv.at[lane_group * 4 + tp],
            j // 16,
            j % 16,
            to_tp,
        )

    def staying():
        return pltpu.make_async_copy(
            packed.at[pl.ds(pl.multiple_of(rank * piece, piece), piece)],
            arrived.at[lane_group, pl.ds(pl.multiple_of(tp * piece, piece), piece)],
            d_recv.at[lane_group * 4 + tp],
        )

    @pl.when(to_tp == tp)
    def _():
        staying().start()

    @pl.when(to_tp != tp)
    def _():
        sending(0).start()

    @pl.loop(1, groups)
    def _(i):
        sending(i).start()

    chosen = place[...].astype(jnp.bfloat16)
    hit = jnp.max(place[...], axis=1, keepdims=True) > 0.5
    prompt_here.wait()
    total = jnp.zeros((tokens, 128), jnp.float32)
    for c in range(8):
        for k in range(4):
            got = arrived.at[c, pl.ds(k * piece, piece)]
            pltpu.make_async_copy(got, got, d_recv.at[c * 4 + k]).wait()
        rows_here = jnp.dot(chosen, arrived[c], preferred_element_type=jnp.float32)
        span = slice(c * columns, (c + 1) * columns)
        x = jnp.where(hit, rows_here, prompt[:, span].astype(jnp.float32))
        stream[:, span] = x.astype(jnp.bfloat16)
        for k in range(0, columns, 128):
            total = total + x[:, k : k + 128] * x[:, k : k + 128]

    def finish():
        for copy in copies + sent:
            copy.wait_send()

        @pl.when(to_tp != tp)
        def _():
            sending(0).wait_send()

        @pl.loop(1, groups)
        def _(i):
            sending(i).wait_send()

    return total, finish


def project_part(eps, total, stream, gain, tables_here, acc, m):
    normed, weights, squares, s_send, s_recv, n_send, n_recv = m
    role, seq, tp = lax.axis_index("role"), lax.axis_index("seq"), lax.axis_index("tp")
    rows, columns = stream.shape
    chunk = columns // CHUNKS
    squares[3] = jnp.broadcast_to(
        jnp.sum(jnp.transpose(total), axis=0, keepdims=True), (8, rows)
    )
    sums = []
    for k, off in enumerate((1, 3, 2)):
        copy = remote(
            squares.at[3], squares.at[k], s_send.at[k], s_recv.at[k], role, seq, (tp + off) % 4
        )
        copy.start()
        sums.append(copy)
    for copy in sums:
        copy.wait()
    whole = squares[0] + squares[1] + (squares[2] + squares[3])
    whole = jnp.broadcast_to(whole[0:1], (128, rows))
    inverse = lax.rsqrt(jnp.transpose(whole) / (4 * columns) + eps)[:, 0:1]

    copies = []

    def send(t, c, off):
        copy = remote(
            normed.at[t, c],
            normed.at[t, c],
            n_send.at[len(copies)],
            n_recv.at[t, c],
            role,
            seq,
            (tp + off + 4) % 4,
        )
        copy.start()
        copies.append(copy)

    def arrive(t, c):
        pltpu.make_async_copy(normed.at[t, c], normed.at[t, c], n_recv.at[t, c]).wait()

    def scale(c):
        span = slice(c * chunk, (c + 1) * chunk)
        x = stream[:, span].astype(jnp.float32)
        normed[tp, c] = (x * inverse * gain[:, span].astype(jnp.float32)).astype(jnp.bfloat16)

    scale(0)
    send(tp, 0, 1)
    scale(2)
    send(tp, 2, -1)
    scale(1)
    send(tp, 1, 1)
    scale(3)
    send(tp, 3, -1)
    send(tp, 2, 1)
    send(tp, 0, -1)
    send(tp, 3, 1)
    send(tp, 1, -1)
    before, after, across = (tp + 3) % 4, (tp + 1) % 4, (tp + 2) % 4

    def multiply(t, c, first=False):
        span = pl.ds(pl.multiple_of(t * columns + c * chunk, chunk), chunk)
        value = jnp.dot(normed[t, c], weights[span, :], preferred_element_type=jnp.float32)
        if first:
            acc[...] = value
        else:
            acc[...] += value

    for copy in tables_here:
        copy.wait()
    for c in range(CHUNKS):
        multiply(tp, c, c == 0)
    for c, d in ((0, 2), (1, 3)):
        arrive(before, c)
        send(before, c, 1)
        arrive(after, d)
        send(after, d, -1)
        multiply(before, c)
        multiply(after, d)
    for c, d in ((2, 0), (3, 1)):
        arrive(before, c)
        multiply(before, c)
        arrive(after, d)
        multiply(after, d)
    for c in (0, 2, 1, 3):
        arrive(across, c)
        multiply(across, c)

    def finish():
        for copy in copies:
            copy.wait_send()

    return finish


def attend_part(q_ref, buf, o_ref, acc, top, total):
    rows = q_ref.shape[0]
    heads = q_ref.shape[1] // HEAD_DIM
    rank = lax.axis_index("role") * lax.axis_size("seq") + lax.axis_index("seq")
    first = rank * rows
    several = KEY_BLOCK // rows
    factor = math.log2(math.e) / math.sqrt(HEAD_DIM)
    acc[...] = jnp.zeros_like(acc)
    total[...] = jnp.zeros_like(total)
    top[...] = jnp.full_like(top, -1e30)

    def block(b, masked):
        got = pl.ds(b * several, several)
        k = buf[got, :, :HEAD_DIM].reshape(KEY_BLOCK, HEAD_DIM)
        v = buf[got, :, HEAD_DIM:].reshape(KEY_BLOCK, HEAD_DIM)
        if masked:
            key_pos = b * KEY_BLOCK + lax.broadcasted_iota(jnp.int32, (rows, KEY_BLOCK), 1)
            query_pos = first + lax.broadcasted_iota(jnp.int32, (rows, KEY_BLOCK), 0)
            visible = key_pos <= query_pos
        for h in range(heads):
            q = q_ref[:, h * HEAD_DIM : (h + 1) * HEAD_DIM]
            s = lax.dot_general(
                q, k, (((1,), (1,)), ((), ())), preferred_element_type=jnp.float32
            )
            if masked:
                s = jnp.where(visible, s, -1e30)
            old = top[h][:, :1]
            new = jnp.maximum(old, jnp.max(s, axis=1, keepdims=True))
            p = jnp.exp2((s - new) * factor)
            alpha = jnp.exp2((old - new) * factor)
            part = p[:, :HEAD_DIM]
            for c in range(1, KEY_BLOCK // HEAD_DIM):
                part = part + p[:, c * HEAD_DIM : (c + 1) * HEAD_DIM]
            total[h] = total[h] * alpha + part
            acc[h] = acc[h] * alpha + jnp.dot(
                p.astype(jnp.bfloat16), v, preferred_element_type=jnp.float32
            )
            top[h] = jnp.broadcast_to(new, (rows, HEAD_DIM))

    full = first // KEY_BLOCK

    @pl.loop(0, full)
    def _(b):
        block(b, False)

    block(full, True)
    for h in range(heads):
        l = jnp.sum(total[h], axis=1, keepdims=True)
        o_ref[:, h * HEAD_DIM : (h + 1) * HEAD_DIM] = (acc[h] / l).astype(o_ref.dtype)


MERGE_SCRATCH = 15
PROJECT_SCRATCH = 7


def kernel(
    hidden,
    merger_out,
    position,
    prompt,
    gain,
    query_weight,
    key_weight,
    value_weight,
    cosine,
    sine,
    stream_out,
    context_out,
    merger_here,
    prompt_here,
    stream,
    queries,
    cosine_here,
    sine_here,
    sums,
    keys,
    k_full,
    k_half,
    k_send,
    acc,
    top,
    total,
    in_sem,
    w_sem,
    *more,
):
    m, p = more[:MERGE_SCRATCH], more[MERGE_SCRATCH:]
    role, seq, tp = lax.axis_index("role"), lax.axis_index("seq"), lax.axis_index("tp")
    rank = role * lax.axis_size("seq") + seq
    rows, width = hidden.shape
    tokens = prompt.shape[0]
    columns = prompt.shape[1]
    heads = query_weight.shape[1] // HEAD_DIM

    fetches = []
    for k, (src, dst) in enumerate(
        (
            (merger_out, merger_here),
            (prompt, prompt_here),
            (cosine, cosine_here),
            (sine, sine_here),
        )
    ):
        copy = pltpu.make_async_copy(src, dst, in_sem.at[k])
        copy.start()
        fetches.append(copy)
    weights = p[1]
    tables_here = []
    for i in range(4):
        for k, (table, spot) in enumerate(
            ((query_weight, 0), (key_weight, heads), (value_weight, heads + 1))
        ):
            span = pl.ds(i * columns, columns)
            lanes = pl.ds(spot * HEAD_DIM, table.shape[1])
            copy = pltpu.make_async_copy(
                table.at[span], weights.at[span, lanes], w_sem.at[i, k]
            )
            copy.start()
            tables_here.append(copy)

    lane = lax.broadcasted_iota(jnp.int32, (rows, 128), 1)
    pos = jnp.transpose(jnp.broadcast_to(position[...], (128, rows)))
    owner = jnp.where(pos >= 0, pos // tokens, -1)
    rest = jnp.where(pos >= 0, pos % tokens, 0)
    code = jnp.where(lane == 0, owner, jnp.where(lane == 1, rest, 0))
    buf = m[0]
    buf[rank, :, :width] = hidden[...]
    buf[rank, :, width:] = code.astype(jnp.float32).astype(jnp.bfloat16)
    greet()
    squares, merged = merge_part(
        hidden, merger_here, position, prompt_here, stream, fetches[0], fetches[1], m
    )
    stream_sent = pltpu.make_async_copy(stream, stream_out, in_sem.at[4])
    stream_sent.start()
    projected = project_part(1e-06, squares, stream, gain, tables_here, sums, p)
    fetches[2].wait()
    fetches[3].wait()

    def turned(h):
        u = sums[:, h * HEAD_DIM : (h + 1) * HEAD_DIM]
        u = u * cosine_here[...] + pltpu.roll(u, HEAD_DIM // 2, 1) * sine_here[...]
        return u.astype(jnp.bfloat16)

    keys[rank, :, :HEAD_DIM] = turned(heads)
    keys[rank, :, HEAD_DIM:] = sums[:, (heads + 1) * HEAD_DIM :].astype(jnp.bfloat16)
    for h in range(heads):
        queries[:, h * HEAD_DIM : (h + 1) * HEAD_DIM] = turned(h)
    k_sent = plane_gather(keys, k_full, k_half, k_send)
    attend_part(queries, keys, context_out, acc, top, total)
    stream_sent.wait()
    for copy in k_sent:
        copy.wait_send()
    projected()
    merged()


def together(hidden, merger_out, position, prompt, gain, wq, wk, wv, cosine, sine):
    rows, width = hidden.shape
    groups = lax.axis_size("role") * lax.axis_size("seq")
    tokens, columns = prompt.shape
    strip = merger_out.shape[1]
    quarter = groups // 4
    slots = groups * quarter * (2 * rows // groups)
    heads = wq.shape[1] // HEAD_DIM
    wide = wq.shape[1] + 2 * HEAD_DIM
    dma = pltpu.SemaphoreType.DMA
    vmem = pl.BlockSpec(memory_space=pltpu.VMEM)
    hbm = pl.BlockSpec(memory_space=pl.ANY)
    bf16, f32 = jnp.bfloat16, jnp.float32
    return pl.pallas_call(
        kernel,
        out_shape=(
            jax.ShapeDtypeStruct(prompt.shape, bf16),
            jax.ShapeDtypeStruct((tokens, wq.shape[1]), bf16),
        ),
        in_specs=[vmem, hbm, vmem, hbm, vmem, hbm, hbm, hbm, hbm, hbm],
        out_specs=(hbm, vmem),
        scratch_shapes=[
            pltpu.VMEM(merger_out.shape, bf16),
            pltpu.VMEM(prompt.shape, bf16),
            pltpu.VMEM(prompt.shape, bf16),
            pltpu.VMEM((tokens, wq.shape[1]), bf16),
            pltpu.VMEM(cosine.shape, f32),
            pltpu.VMEM(sine.shape, f32),
            pltpu.VMEM((tokens, wide), f32),
            pltpu.VMEM((groups, tokens, 2 * HEAD_DIM), bf16),
            dma((groups,)),
            dma((groups, 2)),
            dma((PLANE_SENDS,)),
            pltpu.VMEM((heads, tokens, HEAD_DIM), f32),
            pltpu.VMEM((heads, tokens, HEAD_DIM), f32),
            pltpu.VMEM((heads, tokens, HEAD_DIM), f32),
            dma((5,)),
            dma((4, 3)),
            pltpu.VMEM((groups, rows, width + 128), bf16),
            dma((groups,)),
            dma((groups, 2)),
            dma((PLANE_SENDS,)),
            pltpu.VMEM((8, 3, rows, strip), bf16),
            pltpu.VMEM((3, quarter, rows, strip), bf16),
            pltpu.VMEM((quarter, rows, strip), f32),
            dma((8, 3)),
            dma((3, quarter)),
            pltpu.VMEM((quarter * rows, slots), bf16),
            pltpu.VMEM((tokens, 128), f32),
            pltpu.VMEM((slots, strip), bf16),
            pltpu.VMEM((8, slots // 8, strip), bf16),
            dma((groups,)),
            dma((groups,)),
            pltpu.VMEM((4, CHUNKS, tokens, columns // CHUNKS), bf16),
            pltpu.VMEM((4 * columns, wide), bf16),
            pltpu.VMEM((4, 8, tokens), f32),
            dma((3,)),
            dma((3,)),
            dma((3 * CHUNKS,)),
            dma((4, CHUNKS)),
        ],
        compiler_params=pltpu.CompilerParams(
            has_side_effects=True, vmem_limit_bytes=60 << 20, collective_id=0
        ),
    )(hidden, merger_out, position, prompt, gain, wq, wk, wv, cosine, sine)


def body(
    merger_hidden,
    merger_out,
    row_position,
    prompt_embeds,
    norm_gain,
    query_weight,
    key_weight,
    value_weight,
):
    device_rank = lax.axis_index(("role", "seq"))
    tok_count = prompt_embeds.shape[0]
    positions = device_rank * tok_count + jnp.arange(tok_count, dtype=jnp.int32)
    cosine, sine = rotary(positions)
    stream, context = together(
        merger_hidden,
        merger_out,
        row_position[None, :],
        prompt_embeds,
        norm_gain[None, :],
        query_weight,
        key_weight,
        value_weight,
        cosine,
        sine,
    )
    return (stream, context)


def solution(mesh):
    in_specs = (
        P(("role", "seq"), "tp"),
        P("tp", ("role", "seq")),
        P(("role", "seq")),
        P(("role", "seq"), "tp"),
        P("tp"),
        P(None, "tp"),
        P(None, "tp"),
        P(None, "tp"),
    )
    out_specs = (P(("role", "seq"), "tp"), P(("role", "seq"), "tp"))
    return jax.shard_map(body, mesh=mesh, in_specs=in_specs, out_specs=out_specs, check_vma=False)
```

time: 195 us -> 161 us (0.83)
  Pallas kernels: 183 us -> 154 us
  local copies, waits for them, and re-layouts: 9.25 us -> 4.45 us
    pallas_call x3 -> x1, Pallas kernels: 183 us -> 154 us  [together(): pl.pallas_call(kernel, out_shape=(jax.ShapeDtypeStruct(prompt.shape, bf16...]
    unnamed x18 -> x4, local copies, waits for them, and re-layouts: 7.9 us -> 3.16 us
where the time goes in v4:
time: 161 us; the launch traced here: 160 us
  Pallas kernels  154 us (96%)
  local copies, waits for them, and re-layouts  4.45 us (3%)
    pallas_call x1, Pallas kernels, together(): pl.pallas_call(kernel, out_shape=(jax.ShapeDtypeStruct(prompt.shape, bf16...  154 us

profile of v4, /device:TPU:97, one launch (start us, length us, event | category | flops | bytes accessed | tf_op | source)
XLA Modules:
  0.0 160.4 jit_solution(3518956479136982906)
XLA Ops:
  0.7 1.3 broadcast_in_dim.9.gain
  1.9 0.5 fusion
  2.5 0.8 pad_maximum_fusion
  3.3 153.9 %shard_map.95 = (bf16[256,2048]{1,0:T(8,128)(2,1)}, bf16[256,1024]{1,0:T(8,128)(2,1)}) custom-call(bf16[64,1280]{1,0:T(8,128)(2,1)} %hidden.1, bf16[1280,256]{1,0:T(8,128)(2,1)} %merger_out.1, s32[1,64]{1,0:T(1,128)} %bitcast.1, bf16[256,2048]{1,0:T(8,128)(2,1)} %prompt.1, bf16[1,2048]{1,0:T(2,128)(2,1)} %broadcast_in_dim.9.gain, ...), custom_call_target="tpu_custom_call" | custom-call | tf_op jit(solution)/shard_map/pallas_call | solution.py:609
  157.2 0.0 copy-start
  157.2 2.4 %copy.12 = bf16[256,2048]{1,0:T(8,128)(2,1)} copy(bf16[256,2048]{1,0:T(8,128)(2,1)} %get-tuple-element.9) | data formatting | bytes 2097152
  159.6 0.0 copy-done
  159.6 0.8 copy.13
  (2 shorter events, 0.0 us)
Async XLA Ops:
  157.2 2.4 %copy-start = (bf16[256,1024]{1,0:T(8,128)(2,1)S(1)}, bf16[256,1024]{1,0:T(8,128)(2,1)}, u32[]{:S(2)}) copy-start(bf16[256,1024]{1,0:T(8,128)(2,1)} %get-tuple-element.10) | copy-start | bytes 1572868

commit v5 on v4

--- a/solution.py
+++ b/solution.py
@@ -37,7 +37,7 @@
     )
 
 
-def plane_gather(buf, full_sem, half_sem, send_sem, on_line=None):
+def plane_steps(buf, full_sem, half_sem, send_sem):
     role, seq, tp = lax.axis_index("role"), lax.axis_index("seq"), lax.axis_index("tp")
     step_a, step_b = 1 + 3 * role, 4 - 3 * role
     z, x = seq // SIDE, seq % SIDE
@@ -53,19 +53,17 @@
         return role * (SIDE * SIDE) + seq_of(a, b)
 
     def whole(slot, to_role, to_seq):
-        copy = remote(
+        remote(
             buf.at[slot], buf.at[slot], send_sem.at[len(sent)], full_sem.at[slot], to_role, to_seq, tp
-        )
-        copy.start()
-        sent.append(copy)
+        ).start()
+        sent.append(2 * half)
 
     def part(slot, k, to_seq):
         piece = buf.at[slot, pl.ds(k * half, half)]
-        copy = remote(
+        remote(
             piece, piece, send_sem.at[len(sent)], half_sem.at[slot, k], role, to_seq, tp
-        )
-        copy.start()
-        sent.append(copy)
+        ).start()
+        sent.append(half)
 
     def wait_whole(slot):
         pltpu.make_async_copy(buf.at[slot], buf.at[slot], full_sem.at[slot]).wait()
@@ -79,15 +77,6 @@
         whole(slot, role, seq_of(0, 1))
         whole(slot, role, seq_of(0, -1))
         whole(slot, 1 - role, seq)
-
-    own = slot_of(0, 0)
-    whole(own, role, seq_of(1, 0))
-    whole(own, role, seq_of(-1, 0))
-    spread_b(own)
-    for a, k in ((-1, 0), (1, 1)):
-        wait_whole(slot_of(a, 0))
-        part(slot_of(a, 0), k, seq_of(-a, 0))
-        spread_b(slot_of(a, 0))
 
     def pass_b(a):
         for b, k in ((-1, 0), (1, 1)):
@@ -95,40 +84,62 @@
             part(slot_of(a, b), k, seq_of(0, -b))
             whole(slot_of(a, b), 1 - role, seq)
 
-    def line(b):
-        if on_line is not None:
-            on_line(role, (cb + b + SIDE) % SIDE)
-
-    def other_line(b):
+    def other(b):
         fixed = (ca + b + SIDE) % SIDE
         for k in range(SIDE):
             wait_whole((1 - role) * (SIDE * SIDE) + fixed * step_a + k * step_b)
-        if on_line is not None:
-            on_line(1 - role, fixed)
-
-    pass_b(0)
-    wait_parts(slot_of(2, 0))
-    spread_b(slot_of(2, 0))
-    line(0)
-    for a in (-1, 1):
-        pass_b(a)
-    other_line(0)
-    pass_b(2)
-    line(-1)
-    line(1)
-    other_line(-1)
-    other_line(1)
-    for a in (0, -1, 1, 2):
-        wait_parts(slot_of(a, 2))
-        whole(slot_of(a, 2), 1 - role, seq)
-    line(2)
-    other_line(2)
-    return sent
+
+    def begin():
+        own = slot_of(0, 0)
+        whole(own, role, seq_of(1, 0))
+        whole(own, role, seq_of(-1, 0))
+        spread_b(own)
+        for a, k in ((-1, 0), (1, 1)):
+            wait_whole(slot_of(a, 0))
+            part(slot_of(a, 0), k, seq_of(-a, 0))
+            spread_b(slot_of(a, 0))
+        pass_b(0)
+        wait_parts(slot_of(2, 0))
+        spread_b(slot_of(2, 0))
+
+    def second():
+        pass_b(-1)
+        pass_b(1)
+        other(0)
+
+    def last():
+        for a in (0, -1, 1, 2):
+            wait_parts(slot_of(a, 2))
+            whole(slot_of(a, 2), 1 - role, seq)
+        other(1)
+
+    def mine(b):
+        return role, (cb + b + SIDE) % SIDE
+
+    def theirs(b):
+        return 1 - role, (ca + b + SIDE) % SIDE
+
+    steps = (
+        (begin, mine(0)),
+        (second, theirs(0)),
+        (lambda: pass_b(2), mine(-1)),
+        (lambda: None, mine(1)),
+        (lambda: other(-1), theirs(-1)),
+        (last, theirs(1)),
+        (lambda: None, mine(2)),
+        (lambda: other(2), theirs(2)),
+    )
+
+    def finish():
+        for n, rows in enumerate(sent):
+            piece = buf.at[0, pl.ds(0, rows)]
+            pltpu.make_async_copy(piece, piece, send_sem.at[n]).wait()
+
+    return steps, finish
 
 
 PLANE_SENDS = 2 + 3 * 4 + 2 + 8 + 12
 CHUNKS = 4
-KEY_BLOCK = 1024
 
 
 def iota(shape, dim):
@@ -225,7 +236,10 @@
             copies.append(copy)
         mine[spots[3]] = value[3 * rows :]
 
-    sent = plane_gather(buf, full_sem, half_sem, send_sem, on_line)
+    steps, sent = plane_steps(buf, full_sem, half_sem, send_sem)
+    for step, (of_role, fixed) in steps:
+        step()
+        on_line(of_role, fixed)
 
     r0 = lax.broadcasted_iota(jnp.int32, (some, some), 0)
     r1 = lax.broadcasted_iota(jnp.int32, (some, some), 1)
@@ -330,7 +344,8 @@
             total = total + x[:, k : k + 128] * x[:, k : k + 128]
 
     def finish():
-        for copy in copies + sent:
+        sent()
+        for copy in copies:
             copy.wait_send()
 
         @pl.when(to_tp != tp)
@@ -437,55 +452,77 @@
     return finish
 
 
-def attend_part(q_ref, buf, o_ref, acc, top, total):
-    rows = q_ref.shape[0]
-    heads = q_ref.shape[1] // HEAD_DIM
-    rank = lax.axis_index("role") * lax.axis_size("seq") + lax.axis_index("seq")
-    first = rank * rows
-    several = KEY_BLOCK // rows
+def attend_part(q_ref, buf, o_ref, acc, top, total, scores, bias, sems):
+    heads, rows = q_ref.shape[:2]
+    role, seq = lax.axis_index("role"), lax.axis_index("seq")
+    z, x = seq // SIDE, seq % SIDE
+    rank = role * (SIDE * SIDE) + seq
     factor = math.log2(math.e) / math.sqrt(HEAD_DIM)
+    span = SIDE * rows
     acc[...] = jnp.zeros_like(acc)
     total[...] = jnp.zeros_like(total)
     top[...] = jnp.full_like(top, -1e30)
 
-    def block(b, masked):
-        got = pl.ds(b * several, several)
-        k = buf[got, :, :HEAD_DIM].reshape(KEY_BLOCK, HEAD_DIM)
-        v = buf[got, :, HEAD_DIM:].reshape(KEY_BLOCK, HEAD_DIM)
+    def block(slots, masked):
+        k = jnp.concatenate([buf[slot, :, :HEAD_DIM] for slot in slots], axis=0)
+        v = jnp.concatenate([buf[slot, :, HEAD_DIM:] for slot in slots], axis=0)
         if masked:
-            key_pos = b * KEY_BLOCK + lax.broadcasted_iota(jnp.int32, (rows, KEY_BLOCK), 1)
-            query_pos = first + lax.broadcasted_iota(jnp.int32, (rows, KEY_BLOCK), 0)
-            visible = key_pos <= query_pos
+            ahead = lax.broadcasted_iota(jnp.int32, (rows, rows), 1) - lax.broadcasted_iota(
+                jnp.int32, (rows, rows), 0
+            )
+            for n, slot in enumerate(slots):
+                bias[:, n * rows : (n + 1) * rows] = jnp.where(
+                    ahead <= (rank - slot) * rows, 0.0, -1e30
+                )
+
+        def score(h):
+            scores[h % 2] = lax.dot_general(
+                q_ref[h], k, (((1,), (1,)), ((), ())), preferred_element_type=jnp.float32
+            )
+
+        score(0)
         for h in range(heads):
-            q = q_ref[:, h * HEAD_DIM : (h + 1) * HEAD_DIM]
-            s = lax.dot_general(
-                q, k, (((1,), (1,)), ((), ())), preferred_element_type=jnp.float32
-            )
+            if h + 1 < heads:
+                score(h + 1)
+            s = scores[h % 2]
             if masked:
-                s = jnp.where(visible, s, -1e30)
+                s = s + bias[...]
             old = top[h][:, :1]
             new = jnp.maximum(old, jnp.max(s, axis=1, keepdims=True))
             p = jnp.exp2((s - new) * factor)
             alpha = jnp.exp2((old - new) * factor)
             part = p[:, :HEAD_DIM]
-            for c in range(1, KEY_BLOCK // HEAD_DIM):
-                part = part + p[:, c * HEAD_DIM : (c + 1) * HEAD_DIM]
+            for c in range(HEAD_DIM, span, HEAD_DIM):
+                part = part + p[:, c : c + HEAD_DIM]
             total[h] = total[h] * alpha + part
             acc[h] = acc[h] * alpha + jnp.dot(
                 p.astype(jnp.bfloat16), v, preferred_element_type=jnp.float32
             )
             top[h] = jnp.broadcast_to(new, (rows, HEAD_DIM))
 
-    full = first // KEY_BLOCK
-
-    @pl.loop(0, full)
-    def _(b):
-        block(b, False)
-
-    block(full, True)
+    steps, sent = plane_steps(buf, *sems)
+
+    @pl.loop(0, len(steps))
+    def _(e):
+        for n, (step, _) in enumerate(steps):
+            pl.when(e == n)(step)
+        of_role, fixed = steps[0][1]
+        for n, (_, line) in enumerate(steps):
+            of_role = jnp.where(e == n, line[0], of_role)
+            fixed = jnp.where(e == n, line[1], fixed)
+        step_a, step_b = 1 + 3 * of_role, 4 - 3 * of_role
+        slots = [
+            of_role * (SIDE * SIDE) + along * step_a + fixed * step_b for along in range(SIDE)
+        ]
+        clear = slots[-1] < rank
+        some = slots[0] <= rank
+        pl.when(clear)(lambda: block(slots, False))
+        pl.when(some & jnp.logical_not(clear))(lambda: block(slots, True))
+
     for h in range(heads):
         l = jnp.sum(total[h], axis=1, keepdims=True)
         o_ref[:, h * HEAD_DIM : (h + 1) * HEAD_DIM] = (acc[h] / l).astype(o_ref.dtype)
+    return sent
 
 
 MERGE_SCRATCH = 15
@@ -519,6 +556,8 @@
     acc,
     top,
     total,
+    scores,
+    bias,
     in_sem,
     w_sem,
     *more,
@@ -583,12 +622,12 @@
     keys[rank, :, :HEAD_DIM] = turned(heads)
     keys[rank, :, HEAD_DIM:] = sums[:, (heads + 1) * HEAD_DIM :].astype(jnp.bfloat16)
     for h in range(heads):
-        queries[:, h * HEAD_DIM : (h + 1) * HEAD_DIM] = turned(h)
-    k_sent = plane_gather(keys, k_full, k_half, k_send)
-    attend_part(queries, keys, context_out, acc, top, total)
+        queries[h] = turned(h)
+    k_sent = attend_part(
+        queries, keys, context_out, acc, top, total, scores, bias, (k_full, k_half, k_send)
+    )
     stream_sent.wait()
-    for copy in k_sent:
-        copy.wait_send()
+    k_sent()
     projected()
     merged()
 
@@ -618,7 +657,7 @@
             pltpu.VMEM(merger_out.shape, bf16),
             pltpu.VMEM(prompt.shape, bf16),
             pltpu.VMEM(prompt.shape, bf16),
-            pltpu.VMEM((tokens, wq.shape[1]), bf16),
+            pltpu.VMEM((heads, tokens, HEAD_DIM), bf16),
             pltpu.VMEM(cosine.shape, f32),
             pltpu.VMEM(sine.shape, f32),
             pltpu.VMEM((tokens, wide), f32),
@@ -629,6 +668,8 @@
             pltpu.VMEM((heads, tokens, HEAD_DIM), f32),
             pltpu.VMEM((heads, tokens, HEAD_DIM), f32),
             pltpu.VMEM((heads, tokens, HEAD_DIM), f32),
+            pltpu.VMEM((2, tokens, SIDE * tokens), f32),
+            pltpu.VMEM((tokens, SIDE * tokens), f32),
             dma((5,)),
             dma((4, 3)),
             pltpu.VMEM((groups, rows, width + 128), bf16),

time: 161 us -> 140 us (0.87); the launches traced: 160 us -> 138 us
  Pallas kernels: 154 us -> 131 us
    pallas_call x1, Pallas kernels: 154 us -> 131 us  [together(): pl.pallas_call(kernel, out_shape=(jax.ShapeDtypeStruct(prompt.shape, bf16...]
where the time goes in v5:
time: 140 us; the launch traced here: 138 us
  Pallas kernels  131 us (94%)
  local copies, waits for them, and re-layouts  4.45 us (3%)
    pallas_call x1, Pallas kernels, together(): pl.pallas_call(kernel, out_shape=(jax.ShapeDtypeStruct(prompt.shape, bf16...  131 us
    unnamed x4, local copies, waits for them, and re-layouts  3.16 us

profile of v5, /device:TPU:97, one launch (start us, length us, event | category | flops | bytes accessed | tf_op | source)
XLA Modules:
  0.0 137.6 jit_solution(13928177549424254264)
XLA Ops:
  0.7 1.3 broadcast_in_dim.9.gain
  1.9 0.5 fusion
  2.5 0.8 pad_maximum_fusion
  3.3 131.1 %shard_map.95 = (bf16[256,2048]{1,0:T(8,128)(2,1)}, bf16[256,1024]{1,0:T(8,128)(2,1)}) custom-call(bf16[64,1280]{1,0:T(8,128)(2,1)} %hidden.1, bf16[1280,256]{1,0:T(8,128)(2,1)} %merger_out.1, s32[1,64]{1,0:T(1,128)} %bitcast.1, bf16[256,2048]{1,0:T(8,128)(2,1)} %prompt.1, bf16[1,2048]{1,0:T(2,128)(2,1)} %broadcast_in_dim.9.gain, ...), custom_call_target="tpu_custom_call" | custom-call | tf_op jit(solution)/shard_map/pallas_call | solution.py:648
  134.4 0.0 copy-start
  134.4 2.4 %copy.12 = bf16[256,2048]{1,0:T(8,128)(2,1)} copy(bf16[256,2048]{1,0:T(8,128)(2,1)} %get-tuple-element.9) | data formatting | bytes 2097152
  136.8 0.0 copy-done
  136.8 0.8 copy.13
  (2 shorter events, 0.0 us)
Async XLA Ops:
  134.4 2.4 %copy-start = (bf16[256,1024]{1,0:T(8,128)(2,1)S(1)}, bf16[256,1024]{1,0:T(8,128)(2,1)}, u32[]{:S(2)}) copy-start(bf16[256,1024]{1,0:T(8,128)(2,1)} %get-tuple-element.10) | copy-start | bytes 1572868

commit v6 on v5

--- a/solution.py
+++ b/solution.py
@@ -149,7 +149,6 @@
 def greet():
     role, seq, tp = lax.axis_index("role"), lax.axis_index("seq"), lax.axis_index("tp")
     z, x = seq // SIDE, seq % SIDE
-    rank = role * (SIDE * SIDE) + seq
     barrier = pltpu.get_barrier_semaphore()
 
     def tell(to_role, to_seq, to_tp):
@@ -164,16 +163,7 @@
     for k in (1, 2, 3):
         tell(role, seq, (tp + k) % 4)
 
-    @pl.loop(0, 32)
-    def _(i):
-        source = tp * 8 + i // 4
-
-        @pl.when((source != rank) | (i % 4 != tp))
-        def _():
-            tell(source // 16, source % 16, i % 4)
-
-    self_too = jnp.where(rank // 8 == tp, 1, 0)
-    pl.semaphore_wait(barrier, 40 - self_too)
+    pl.semaphore_wait(barrier, 8)
 
 
 def merge_part(
@@ -540,11 +530,10 @@
     value_weight,
     cosine,
     sine,
-    stream_out,
+    stream,
     context_out,
     merger_here,
     prompt_here,
-    stream,
     queries,
     cosine_here,
     sine_here,
@@ -608,8 +597,6 @@
     squares, merged = merge_part(
         hidden, merger_here, position, prompt_here, stream, fetches[0], fetches[1], m
     )
-    stream_sent = pltpu.make_async_copy(stream, stream_out, in_sem.at[4])
-    stream_sent.start()
     projected = project_part(1e-06, squares, stream, gain, tables_here, sums, p)
     fetches[2].wait()
     fetches[3].wait()
@@ -626,7 +613,6 @@
     k_sent = attend_part(
         queries, keys, context_out, acc, top, total, scores, bias, (k_full, k_half, k_send)
     )
-    stream_sent.wait()
     k_sent()
     projected()
     merged()
@@ -652,10 +638,9 @@
             jax.ShapeDtypeStruct((tokens, wq.shape[1]), bf16),
         ),
         in_specs=[vmem, hbm, vmem, hbm, vmem, hbm, hbm, hbm, hbm, hbm],
-        out_specs=(hbm, vmem),
+        out_specs=(vmem, vmem),
         scratch_shapes=[
             pltpu.VMEM(merger_out.shape, bf16),
-            pltpu.VMEM(prompt.shape, bf16),
             pltpu.VMEM(prompt.shape, bf16),
             pltpu.VMEM((heads, tokens, HEAD_DIM), bf16),
             pltpu.VMEM(cosine.shape, f32),
@@ -670,7 +655,7 @@
             pltpu.VMEM((heads, tokens, HEAD_DIM), f32),
             pltpu.VMEM((2, tokens, SIDE * tokens), f32),
             pltpu.VMEM((tokens, SIDE * tokens), f32),
-            dma((5,)),
+            dma((4,)),
             dma((4, 3)),
             pltpu.VMEM((groups, rows, width + 128), bf16),
             dma((groups,)),

time: 140 us -> 138 us (0.986)
  no operation moved by 1% of the time
where the time goes in v6:
time: 138 us; the launch traced here: 137 us
  Pallas kernels  130 us (94%)
  local copies, waits for them, and re-layouts  4.45 us (3%)
  other arithmetic  1.39 us (1%)
    pallas_call x1, Pallas kernels, together(): pl.pallas_call(kernel, out_shape=(jax.ShapeDtypeStruct(prompt.shape, bf16...  130 us
    unnamed x4, local copies, waits for them, and re-layouts  3.16 us

profile of v6, /device:TPU:97, one launch (start us, length us, event | category | flops | bytes accessed | tf_op | source)
XLA Modules:
  0.0 136.8 jit_solution(3473184950707189360)
XLA Ops:
  0.7 1.3 broadcast_in_dim.9.gain
  1.9 0.5 fusion
  2.5 0.8 pad_maximum_fusion
  3.3 130.3 %shard_map.95 = (bf16[256,2048]{1,0:T(8,128)(2,1)}, bf16[256,1024]{1,0:T(8,128)(2,1)}) custom-call(bf16[64,1280]{1,0:T(8,128)(2,1)} %hidden.1, bf16[1280,256]{1,0:T(8,128)(2,1)} %merger_out.1, s32[1,64]{1,0:T(1,128)} %bitcast.1, bf16[256,2048]{1,0:T(8,128)(2,1)} %prompt.1, bf16[1,2048]{1,0:T(2,128)(2,1)} %broadcast_in_dim.9.gain, ...), custom_call_target="tpu_custom_call" | custom-call | tf_op jit(solution)/shard_map/pallas_call | solution.py:634
  133.6 0.0 copy-start
  133.6 2.4 %copy.12 = bf16[256,2048]{1,0:T(8,128)(2,1)} copy(bf16[256,2048]{1,0:T(8,128)(2,1)} %get-tuple-element.9) | data formatting | bytes 2097152
  136.0 0.0 copy-done
  136.0 0.8 copy.13
  (2 shorter events, 0.0 us)
Async XLA Ops:
  133.6 2.4 %copy-start = (bf16[256,1024]{1,0:T(8,128)(2,1)S(1)}, bf16[256,1024]{1,0:T(8,128)(2,1)}, u32[]{:S(2)}) copy-start(bf16[256,1024]{1,0:T(8,128)(2,1)} %get-tuple-element.10) | copy-start | bytes 1572868

commit v7 on v6

--- a/solution.py
+++ b/solution.py
@@ -89,15 +89,19 @@
         for k in range(SIDE):
             wait_whole((1 - role) * (SIDE * SIDE) + fixed * step_a + k * step_b)
 
-    def begin():
+    def start():
         own = slot_of(0, 0)
         whole(own, role, seq_of(1, 0))
         whole(own, role, seq_of(-1, 0))
         spread_b(own)
+
+    def along():
         for a, k in ((-1, 0), (1, 1)):
             wait_whole(slot_of(a, 0))
             part(slot_of(a, 0), k, seq_of(-a, 0))
             spread_b(slot_of(a, 0))
+
+    def first():
         pass_b(0)
         wait_parts(slot_of(2, 0))
         spread_b(slot_of(2, 0))
@@ -120,7 +124,9 @@
         return 1 - role, (ca + b + SIDE) % SIDE
 
     steps = (
-        (begin, mine(0)),
+        (start, None),
+        (along, None),
+        (first, mine(0)),
         (second, theirs(0)),
         (lambda: pass_b(2), mine(-1)),
         (lambda: None, mine(1)),
@@ -227,9 +233,10 @@
         mine[spots[3]] = value[3 * rows :]
 
     steps, sent = plane_steps(buf, full_sem, half_sem, send_sem)
-    for step, (of_role, fixed) in steps:
+    for step, line in steps:
         step()
-        on_line(of_role, fixed)
+        if line is not None:
+            on_line(*line)
 
     r0 = lax.broadcasted_iota(jnp.int32, (some, some), 0)
     r1 = lax.broadcasted_iota(jnp.int32, (some, some), 1)
@@ -353,7 +360,8 @@
     normed, weights, squares, s_send, s_recv, n_send, n_recv = m
     role, seq, tp = lax.axis_index("role"), lax.axis_index("seq"), lax.axis_index("tp")
     rows, columns = stream.shape
-    chunk = columns // CHUNKS
+    chunk = columns // 2
+    few = rows // 2
     squares[3] = jnp.broadcast_to(
         jnp.sum(jnp.transpose(total), axis=0, keepdims=True), (8, rows)
     )
@@ -370,149 +378,157 @@
     whole = jnp.broadcast_to(whole[0:1], (128, rows))
     inverse = lax.rsqrt(jnp.transpose(whole) / (4 * columns) + eps)[:, 0:1]
 
-    copies = []
-
-    def send(t, c, off):
-        copy = remote(
-            normed.at[t, c],
-            normed.at[t, c],
-            n_send.at[len(copies)],
-            n_recv.at[t, c],
+    sent = []
+
+    def send(t, hf, c, off):
+        remote(
+            normed.at[t, hf, c],
+            normed.at[t, hf, c],
+            n_send.at[len(sent)],
+            n_recv.at[t, 2 * hf + c],
             role,
             seq,
             (tp + off + 4) % 4,
-        )
-        copy.start()
-        copies.append(copy)
-
-    def arrive(t, c):
-        pltpu.make_async_copy(normed.at[t, c], normed.at[t, c], n_recv.at[t, c]).wait()
-
-    def scale(c):
+        ).start()
+        sent.append(off)
+
+    def arrive(t, hf, c):
+        got = normed.at[t, hf, c]
+        pltpu.make_async_copy(got, got, n_recv.at[t, 2 * hf + c]).wait()
+
+    def scale(hf, c):
         span = slice(c * chunk, (c + 1) * chunk)
-        x = stream[:, span].astype(jnp.float32)
-        normed[tp, c] = (x * inverse * gain[:, span].astype(jnp.float32)).astype(jnp.bfloat16)
-
-    scale(0)
-    send(tp, 0, 1)
-    scale(2)
-    send(tp, 2, -1)
-    scale(1)
-    send(tp, 1, 1)
-    scale(3)
-    send(tp, 3, -1)
-    send(tp, 2, 1)
-    send(tp, 0, -1)
-    send(tp, 3, 1)
-    send(tp, 1, -1)
+        part = slice(hf * few, (hf + 1) * few)
+        x = stream[part, span].astype(jnp.float32)
+        normed[tp, hf, c] = (
+            x * inverse[part] * gain[:, span].astype(jnp.float32)
+        ).astype(jnp.bfloat16)
+
     before, after, across = (tp + 3) % 4, (tp + 1) % 4, (tp + 2) % 4
 
-    def multiply(t, c, first=False):
+    def multiply(t, hf, c, first=False):
         span = pl.ds(pl.multiple_of(t * columns + c * chunk, chunk), chunk)
-        value = jnp.dot(normed[t, c], weights[span, :], preferred_element_type=jnp.float32)
+        part = slice(hf * few, (hf + 1) * few)
+        value = jnp.dot(normed[t, hf, c], weights[span, :], preferred_element_type=jnp.float32)
         if first:
-            acc[...] = value
+            acc[part, :] = value
         else:
-            acc[...] += value
-
+            acc[part, :] += value
+
+    def send_own(hf):
+        send(tp, hf, 0, 1)
+        send(tp, hf, 1, -1)
+        send(tp, hf, 1, 1)
+        send(tp, hf, 0, -1)
+
+    def near(hf):
+        arrive(before, hf, 0)
+        send(before, hf, 0, 1)
+        arrive(after, hf, 1)
+        send(after, hf, 1, -1)
+        if hf == 0:
+            send_own(1)
+        multiply(before, hf, 0)
+        multiply(after, hf, 1)
+
+    def rest(hf):
+        arrive(before, hf, 1)
+        multiply(before, hf, 1)
+        arrive(after, hf, 0)
+        multiply(after, hf, 0)
+        for c in range(2):
+            arrive(across, hf, c)
+            multiply(across, hf, c)
+
+    scale(0, 0)
+    scale(0, 1)
+    send_own(0)
+    scale(1, 0)
+    scale(1, 1)
     for copy in tables_here:
         copy.wait()
-    for c in range(CHUNKS):
-        multiply(tp, c, c == 0)
-    for c, d in ((0, 2), (1, 3)):
-        arrive(before, c)
-        send(before, c, 1)
-        arrive(after, d)
-        send(after, d, -1)
-        multiply(before, c)
-        multiply(after, d)
-    for c, d in ((2, 0), (3, 1)):
-        arrive(before, c)
-        multiply(before, c)
-        arrive(after, d)
-        multiply(after, d)
-    for c in (0, 2, 1, 3):
-        arrive(across, c)
-        multiply(across, c)
+    for hf in range(2):
+        for c in range(2):
+            multiply(tp, hf, c, c == 0)
+    near(0)
+    rest(0)
 
     def finish():
-        for copy in copies:
-            copy.wait_send()
-
-    return finish
-
-
-def attend_part(q_ref, buf, o_ref, acc, top, total, scores, bias, sems):
+        for n in range(len(sent)):
+            piece = normed.at[0, 0, 0]
+            pltpu.make_async_copy(piece, piece, n_send.at[n]).wait()
+
+    return near, rest, finish
+
+
+def line_slots(of_role, fixed):
+    step_a, step_b = 1 + 3 * of_role, 4 - 3 * of_role
+    return [of_role * (SIDE * SIDE) + n * step_a + fixed * step_b for n in range(SIDE)]
+
+
+def attend_to(q_ref, buf, hf, slots, part, acc, top, total, scores, bias, rank):
     heads, rows = q_ref.shape[:2]
-    role, seq = lax.axis_index("role"), lax.axis_index("seq")
-    z, x = seq // SIDE, seq % SIDE
-    rank = role * (SIDE * SIDE) + seq
+    few = buf.shape[1]
+    count = part.stop - part.start
+    span = len(slots) * few
     factor = math.log2(math.e) / math.sqrt(HEAD_DIM)
-    span = SIDE * rows
-    acc[...] = jnp.zeros_like(acc)
-    total[...] = jnp.zeros_like(total)
-    top[...] = jnp.full_like(top, -1e30)
-
-    def block(slots, masked):
+    low, high = slots[0], slots[0]
+    for slot in slots[1:]:
+        low, high = jnp.minimum(low, slot), jnp.maximum(high, slot)
+
+    def block(masked):
         k = jnp.concatenate([buf[slot, :, :HEAD_DIM] for slot in slots], axis=0)
         v = jnp.concatenate([buf[slot, :, HEAD_DIM:] for slot in slots], axis=0)
         if masked:
-            ahead = lax.broadcasted_iota(jnp.int32, (rows, rows), 1) - lax.broadcasted_iota(
-                jnp.int32, (rows, rows), 0
+            ahead = lax.broadcasted_iota(jnp.int32, (count, few), 1) - lax.broadcasted_iota(
+                jnp.int32, (count, few), 0
             )
             for n, slot in enumerate(slots):
-                bias[:, n * rows : (n + 1) * rows] = jnp.where(
-                    ahead <= (rank - slot) * rows, 0.0, -1e30
+                bias[:count, n * few : (n + 1) * few] = jnp.where(
+                    ahead <= (rank - slot) * rows + part.start - hf * few, 0.0, -1e30
                 )
 
         def score(h):
-            scores[h % 2] = lax.dot_general(
-                q_ref[h], k, (((1,), (1,)), ((), ())), preferred_element_type=jnp.float32
+            scores[h % 2, :count] = lax.dot_general(
+                q_ref[h, part], k, (((1,), (1,)), ((), ())), preferred_element_type=jnp.float32
             )
 
         score(0)
         for h in range(heads):
             if h + 1 < heads:
                 score(h + 1)
-            s = scores[h % 2]
+            s = scores[h % 2, :count]
             if masked:
-                s = s + bias[...]
-            old = top[h][:, :1]
+                s = s + bias[:count]
+            old = top[h, part][:, :1]
             new = jnp.maximum(old, jnp.max(s, axis=1, keepdims=True))
             p = jnp.exp2((s - new) * factor)
             alpha = jnp.exp2((old - new) * factor)
-            part = p[:, :HEAD_DIM]
+            some = p[:, :HEAD_DIM]
             for c in range(HEAD_DIM, span, HEAD_DIM):
-                part = part + p[:, c : c + HEAD_DIM]
-            total[h] = total[h] * alpha + part
-            acc[h] = acc[h] * alpha + jnp.dot(
+                some = some + p[:, c : c + HEAD_DIM]
+            total[h, part] = total[h, part] * alpha + some
+            acc[h, part] = acc[h, part] * alpha + jnp.dot(
                 p.astype(jnp.bfloat16), v, preferred_element_type=jnp.float32
             )
-            top[h] = jnp.broadcast_to(new, (rows, HEAD_DIM))
-
-    steps, sent = plane_steps(buf, *sems)
-
+            top[h, part] = jnp.broadcast_to(new, (count, HEAD_DIM))
+
+    pl.when(high < rank)(lambda: block(False))
+    pl.when((low <= rank) & (high >= rank))(lambda: block(True))
+
+
+def in_steps(steps, visit, extra=()):
     @pl.loop(0, len(steps))
     def _(e):
         for n, (step, _) in enumerate(steps):
             pl.when(e == n)(step)
-        of_role, fixed = steps[0][1]
-        for n, (_, line) in enumerate(steps):
-            of_role = jnp.where(e == n, line[0], of_role)
-            fixed = jnp.where(e == n, line[1], fixed)
-        step_a, step_b = 1 + 3 * of_role, 4 - 3 * of_role
-        slots = [
-            of_role * (SIDE * SIDE) + along * step_a + fixed * step_b for along in range(SIDE)
-        ]
-        clear = slots[-1] < rank
-        some = slots[0] <= rank
-        pl.when(clear)(lambda: block(slots, False))
-        pl.when(some & jnp.logical_not(clear))(lambda: block(slots, True))
-
-    for h in range(heads):
-        l = jnp.sum(total[h], axis=1, keepdims=True)
-        o_ref[:, h * HEAD_DIM : (h + 1) * HEAD_DIM] = (acc[h] / l).astype(o_ref.dtype)
-    return sent
+        of_role, fixed = steps[2][1]
+        for n, (_, line) in enumerate(steps[2:]):
+            of_role = jnp.where(e == n + 2, line[0], of_role)
+            fixed = jnp.where(e == n + 2, line[1], fixed)
+        visit(e, of_role, fixed)
+        for n, act in extra:
+            pl.when(e == n)(act)
 
 
 MERGE_SCRATCH = 15
@@ -538,7 +554,8 @@
     cosine_here,
     sine_here,
     sums,
-    keys,
+    keys_0,
+    keys_1,
     k_full,
     k_half,
     k_send,
@@ -547,6 +564,8 @@
     total,
     scores,
     bias,
+    long_scores,
+    long_bias,
     in_sem,
     w_sem,
     *more,
@@ -597,23 +616,67 @@
     squares, merged = merge_part(
         hidden, merger_here, position, prompt_here, stream, fetches[0], fetches[1], m
     )
-    projected = project_part(1e-06, squares, stream, gain, tables_here, sums, p)
+    near, rest, projected = project_part(1e-06, squares, stream, gain, tables_here, sums, p)
     fetches[2].wait()
     fetches[3].wait()
 
-    def turned(h):
-        u = sums[:, h * HEAD_DIM : (h + 1) * HEAD_DIM]
-        u = u * cosine_here[...] + pltpu.roll(u, HEAD_DIM // 2, 1) * sine_here[...]
-        return u.astype(jnp.bfloat16)
-
-    keys[rank, :, :HEAD_DIM] = turned(heads)
-    keys[rank, :, HEAD_DIM:] = sums[:, (heads + 1) * HEAD_DIM :].astype(jnp.bfloat16)
+    few = tokens // 2
+    state = (acc, top, total)
+    acc[...] = jnp.zeros_like(acc)
+    total[...] = jnp.zeros_like(total)
+    top[...] = jnp.full_like(top, -1e30)
+    halves = (slice(0, few), slice(few, tokens))
+
+    def rotated(hf):
+        part = halves[hf]
+
+        def turned(h):
+            u = sums[part, h * HEAD_DIM : (h + 1) * HEAD_DIM]
+            u = u * cosine_here[part] + pltpu.roll(u, HEAD_DIM // 2, 1) * sine_here[part]
+            return u.astype(jnp.bfloat16)
+
+        keys[hf][rank, :, :HEAD_DIM] = turned(heads)
+        keys[hf][rank, :, HEAD_DIM:] = sums[part, (heads + 1) * HEAD_DIM :].astype(jnp.bfloat16)
+        for h in range(heads):
+            queries[h, part] = turned(h)
+
+    keys = (keys_0, keys_1)
+    rotated(0)
+    steps, sent_0 = plane_steps(keys_0, k_full.at[0], k_half.at[0], k_send.at[0])
+
+    def visit_0(e, of_role, fixed):
+        @pl.when(e >= 2)
+        def _():
+            attend_to(
+                queries, keys_0, 0, line_slots(of_role, fixed), halves[0], *state, scores, bias, rank
+            )
+
+    in_steps(steps, visit_0, ((2, lambda: near(1)),))
+    rest(1)
+    rotated(1)
+    steps, sent_1 = plane_steps(keys_1, k_full.at[1], k_half.at[1], k_send.at[1])
+    everyone = slice(0, tokens)
+
+    def visit_1(e, of_role, fixed):
+        @pl.when(e < 4)
+        def _():
+            slots = line_slots(e // 2, 2 * (e % 2)) + line_slots(e // 2, 2 * (e % 2) + 1)
+            attend_to(
+                queries, keys_0, 0, slots, halves[1], *state, long_scores, long_bias, rank
+            )
+
+        @pl.when(e >= 2)
+        def _():
+            attend_to(
+                queries, keys_1, 1, line_slots(of_role, fixed), everyone, *state, scores, bias, rank
+            )
+
+    in_steps(steps, visit_1)
     for h in range(heads):
-        queries[h] = turned(h)
-    k_sent = attend_part(
-        queries, keys, context_out, acc, top, total, scores, bias, (k_full, k_half, k_send)
-    )
-    k_sent()
+        l = jnp.sum(total[h], axis=1, keepdims=True)
+        context_out[:, h * HEAD_DIM : (h + 1) * HEAD_DIM] = (acc[h] / l).astype(context_out.dtype)
+    sent_0()
+    sent_1()
     projected()
     merged()
 
@@ -646,15 +709,18 @@
             pltpu.VMEM(cosine.shape, f32),
             pltpu.VMEM(sine.shape, f32),
             pltpu.VMEM((tokens, wide), f32),
-            pltpu.VMEM((groups, tokens, 2 * HEAD_DIM), bf16),
-            dma((groups,)),
-            dma((groups, 2)),
-            dma((PLANE_SENDS,)),
+            pltpu.VMEM((groups, tokens // 2, 2 * HEAD_DIM), bf16),
+            pltpu.VMEM((groups, tokens // 2, 2 * HEAD_DIM), bf16),
+            dma((2, groups)),
+            dma((2, groups, 2)),
+            dma((2, PLANE_SENDS)),
             pltpu.VMEM((heads, tokens, HEAD_DIM), f32),
             pltpu.VMEM((heads, tokens, HEAD_DIM), f32),
             pltpu.VMEM((heads, tokens, HEAD_DIM), f32),
-            pltpu.VMEM((2, tokens, SIDE * tokens), f32),
-            pltpu.VMEM((tokens, SIDE * tokens), f32),
+            pltpu.VMEM((2, tokens, SIDE * tokens // 2), f32),
+            pltpu.VMEM((tokens, SIDE * tokens // 2), f32),
+            pltpu.VMEM((2, tokens // 2, SIDE * tokens), f32),
+            pltpu.VMEM((tokens // 2, SIDE * tokens), f32),
             dma((4,)),
             dma((4, 3)),
             pltpu.VMEM((groups, rows, width + 128), bf16),
@@ -672,7 +738,7 @@
             pltpu.VMEM((8, slots // 8, strip), bf16),
             dma((groups,)),
             dma((groups,)),
-            pltpu.VMEM((4, CHUNKS, tokens, columns // CHUNKS), bf16),
+            pltpu.VMEM((4, 2, 2, tokens // 2, columns // 2), bf16),
             pltpu.VMEM((4 * columns, wide), bf16),
             pltpu.VMEM((4, 8, tokens), f32),
             dma((3,)),

time: 138 us -> 151 us (1.094)
  Pallas kernels: 130 us -> 144 us
    pallas_call x1, Pallas kernels: 130 us -> 144 us  [together(): pl.pallas_call(kernel, out_shape=(jax.ShapeDtypeStruct(prompt.shape, bf16...]
where the time goes in v7:
time: 151 us; the launch traced here: 150 us
  Pallas kernels  144 us (95%)
  local copies, waits for them, and re-layouts  4.45 us (3%)
    pallas_call x1, Pallas kernels, together(): pl.pallas_call(kernel, out_shape=(jax.ShapeDtypeStruct(prompt.shape, bf16...  144 us
    unnamed x4, local copies, waits for them, and re-layouts  3.16 us

profile of v7, /device:TPU:97, one launch (start us, length us, event | category | flops | bytes accessed | tf_op | source)
XLA Modules:
  0.0 150.1 jit_solution(3340622803874253058)
XLA Ops:
  0.7 1.3 broadcast_in_dim.9.gain
  1.9 0.5 fusion
  2.5 0.8 pad_maximum_fusion
  3.3 143.6 %shard_map.95 = (bf16[256,2048]{1,0:T(8,128)(2,1)}, bf16[256,1024]{1,0:T(8,128)(2,1)}) custom-call(bf16[64,1280]{1,0:T(8,128)(2,1)} %hidden.1, bf16[1280,256]{1,0:T(8,128)(2,1)} %merger_out.1, s32[1,64]{1,0:T(1,128)} %bitcast.1, bf16[256,2048]{1,0:T(8,128)(2,1)} %prompt.1, bf16[1,2048]{1,0:T(2,128)(2,1)} %broadcast_in_dim.9.gain, ...), custom_call_target="tpu_custom_call" | custom-call | tf_op jit(solution)/shard_map/pallas_call | solution.py:697
  146.9 0.0 copy-start
  146.9 2.4 %copy.12 = bf16[256,2048]{1,0:T(8,128)(2,1)} copy(bf16[256,2048]{1,0:T(8,128)(2,1)} %get-tuple-element.9) | data formatting | bytes 2097152
  149.3 0.0 copy-done
  149.3 0.8 copy.13
  (2 shorter events, 0.0 us)
Async XLA Ops:
  146.9 2.4 %copy-start = (bf16[256,1024]{1,0:T(8,128)(2,1)S(1)}, bf16[256,1024]{1,0:T(8,128)(2,1)}, u32[]{:S(2)}) copy-start(bf16[256,1024]{1,0:T(8,128)(2,1)} %get-tuple-element.10) | copy-start | bytes 1572868

commit v8 on v6

--- a/solution.py
+++ b/solution.py
@@ -16,10 +16,7 @@
     frequency = 1000000.0 ** (-jnp.arange(half_dim, dtype=jnp.float32) / half_dim)
     angles = positions.astype(jnp.float32)[:, None] * frequency[None, :]
     cosine, sine = jnp.cos(angles), jnp.sin(angles)
-    return (
-        jnp.concatenate([cosine, cosine], axis=1),
-        jnp.concatenate([-sine, sine], axis=1),
-    )
+    return cosine, sine
 
 
 MESH = pl.DeviceIdType.MESH
@@ -89,15 +86,19 @@
         for k in range(SIDE):
             wait_whole((1 - role) * (SIDE * SIDE) + fixed * step_a + k * step_b)
 
-    def begin():
+    def start():
         own = slot_of(0, 0)
         whole(own, role, seq_of(1, 0))
         whole(own, role, seq_of(-1, 0))
         spread_b(own)
+
+    def along():
         for a, k in ((-1, 0), (1, 1)):
             wait_whole(slot_of(a, 0))
             part(slot_of(a, 0), k, seq_of(-a, 0))
             spread_b(slot_of(a, 0))
+
+    def first():
         pass_b(0)
         wait_parts(slot_of(2, 0))
         spread_b(slot_of(2, 0))
@@ -120,7 +121,9 @@
         return 1 - role, (ca + b + SIDE) % SIDE
 
     steps = (
-        (begin, mine(0)),
+        (start, None),
+        (along, None),
+        (first, mine(0)),
         (second, theirs(0)),
         (lambda: pass_b(2), mine(-1)),
         (lambda: None, mine(1)),
@@ -227,9 +230,10 @@
         mine[spots[3]] = value[3 * rows :]
 
     steps, sent = plane_steps(buf, full_sem, half_sem, send_sem)
-    for step, (of_role, fixed) in steps:
+    for step, line in steps:
         step()
-        on_line(of_role, fixed)
+        if line is not None:
+            on_line(*line)
 
     r0 = lax.broadcasted_iota(jnp.int32, (some, some), 0)
     r1 = lax.broadcasted_iota(jnp.int32, (some, some), 1)
@@ -349,7 +353,7 @@
     return total, finish
 
 
-def project_part(eps, total, stream, gain, tables_here, acc, m):
+def project_part(eps, total, stream, gain, tables_here, acc, meanwhile, m):
     normed, weights, squares, s_send, s_recv, n_send, n_recv = m
     role, seq, tp = lax.axis_index("role"), lax.axis_index("seq"), lax.axis_index("tp")
     rows, columns = stream.shape
@@ -364,6 +368,7 @@
         )
         copy.start()
         sums.append(copy)
+    meanwhile()
     for copy in sums:
         copy.wait()
     whole = squares[0] + squares[1] + (squares[2] + squares[3])
@@ -391,7 +396,7 @@
     def scale(c):
         span = slice(c * chunk, (c + 1) * chunk)
         x = stream[:, span].astype(jnp.float32)
-        normed[tp, c] = (x * inverse * gain[:, span].astype(jnp.float32)).astype(jnp.bfloat16)
+        normed[tp, c] = (x * inverse * gain[span].astype(jnp.float32).reshape(1, chunk)).astype(jnp.bfloat16)
 
     scale(0)
     send(tp, 0, 1)
@@ -442,16 +447,13 @@
     return finish
 
 
-def attend_part(q_ref, buf, o_ref, acc, top, total, scores, bias, sems):
+def attend_part(q_ref, buf, o_ref, acc, top, total, scores, bias, steps):
     heads, rows = q_ref.shape[:2]
     role, seq = lax.axis_index("role"), lax.axis_index("seq")
     z, x = seq // SIDE, seq % SIDE
     rank = role * (SIDE * SIDE) + seq
     factor = math.log2(math.e) / math.sqrt(HEAD_DIM)
     span = SIDE * rows
-    acc[...] = jnp.zeros_like(acc)
-    total[...] = jnp.zeros_like(total)
-    top[...] = jnp.full_like(top, -1e30)
 
     def block(slots, masked):
         k = jnp.concatenate([buf[slot, :, :HEAD_DIM] for slot in slots], axis=0)
@@ -490,8 +492,6 @@
             )
             top[h] = jnp.broadcast_to(new, (rows, HEAD_DIM))
 
-    steps, sent = plane_steps(buf, *sems)
-
     @pl.loop(0, len(steps))
     def _(e):
         for n, (step, _) in enumerate(steps):
@@ -512,7 +512,6 @@
     for h in range(heads):
         l = jnp.sum(total[h], axis=1, keepdims=True)
         o_ref[:, h * HEAD_DIM : (h + 1) * HEAD_DIM] = (acc[h] / l).astype(o_ref.dtype)
-    return sent
 
 
 MERGE_SCRATCH = 15
@@ -597,22 +596,32 @@
     squares, merged = merge_part(
         hidden, merger_here, position, prompt_here, stream, fetches[0], fetches[1], m
     )
-    projected = project_part(1e-06, squares, stream, gain, tables_here, sums, p)
+
+    def clear():
+        acc[...] = jnp.zeros_like(acc)
+        total[...] = jnp.zeros_like(total)
+        top[...] = jnp.full_like(top, -1e30)
+
+    projected = project_part(1e-06, squares, stream, gain, tables_here, sums, clear, p)
     fetches[2].wait()
     fetches[3].wait()
 
+    cosine_wide = jnp.concatenate([cosine_here[...], cosine_here[...]], axis=1)
+    sine_wide = jnp.concatenate([-sine_here[...], sine_here[...]], axis=1)
+
     def turned(h):
         u = sums[:, h * HEAD_DIM : (h + 1) * HEAD_DIM]
-        u = u * cosine_here[...] + pltpu.roll(u, HEAD_DIM // 2, 1) * sine_here[...]
+        u = u * cosine_wide + pltpu.roll(u, HEAD_DIM // 2, 1) * sine_wide
         return u.astype(jnp.bfloat16)
 
     keys[rank, :, :HEAD_DIM] = turned(heads)
     keys[rank, :, HEAD_DIM:] = sums[:, (heads + 1) * HEAD_DIM :].astype(jnp.bfloat16)
+    steps, k_sent = plane_steps(keys, k_full, k_half, k_send)
+    steps[0][0]()
     for h in range(heads):
         queries[h] = turned(h)
-    k_sent = attend_part(
-        queries, keys, context_out, acc, top, total, scores, bias, (k_full, k_half, k_send)
-    )
+    steps[1][0]()
+    attend_part(queries, keys, context_out, acc, top, total, scores, bias, steps[2:])
     k_sent()
     projected()
     merged()
@@ -705,7 +714,7 @@
         merger_out,
         row_position[None, :],
         prompt_embeds,
-        norm_gain[None, :],
+        norm_gain,
         query_weight,
         key_weight,
         value_weight,

time: 138 us -> 136 us (0.986)
  no operation moved by 1% of the time
where the time goes in v8:
time: 136 us; the launch traced here: 135 us
  Pallas kernels  130 us (96%)
  local copies, waits for them, and re-layouts  3.16 us (2%)
    pallas_call x1, Pallas kernels, together(): pl.pallas_call(kernel, out_shape=(jax.ShapeDtypeStruct(prompt.shape, bf16...  130 us
    unnamed x4, local copies, waits for them, and re-layouts  3.16 us

profile of v8, /device:TPU:97, one launch (start us, length us, event | category | flops | bytes accessed | tf_op | source)
XLA Modules:
  0.0 135.2 jit_solution(4417963113130890087)
XLA Ops:
  0.7 1.2 multiply_sine_fusion
  1.9 130.1 %shard_map.95 = (bf16[256,2048]{1,0:T(8,128)(2,1)}, bf16[256,1024]{1,0:T(8,128)(2,1)}) custom-call(bf16[64,1280]{1,0:T(8,128)(2,1)} %hidden.1, bf16[1280,256]{1,0:T(8,128)(2,1)} %merger_out.1, s32[1,64]{1,0:T(1,128)} %bitcast.1, bf16[256,2048]{1,0:T(8,128)(2,1)} %prompt.1, bf16[2048]{0:T(1024)(128)(2,1)} %gain.1, bf16[8192,1024]{1,0:T(8,128)(2,1)} %query_weight.1, ...), custom_call_target="tpu_custom_call" | custom-call | tf_op jit(solution)/shard_map/pallas_call | solution.py:643
  132.0 0.0 copy-start
  132.0 2.4 %copy.12 = bf16[256,2048]{1,0:T(8,128)(2,1)} copy(bf16[256,2048]{1,0:T(8,128)(2,1)} %get-tuple-element.6) | data formatting | bytes 2097152
  134.4 0.0 copy-done
  134.4 0.8 copy.13
  (2 shorter events, 0.0 us)
Async XLA Ops:
  132.0 2.4 %copy-start = (bf16[256,1024]{1,0:T(8,128)(2,1)S(1)}, bf16[256,1024]{1,0:T(8,128)(2,1)}, u32[]{:S(2)}) copy-start(bf16[256,1024]{1,0:T(8,128)(2,1)} %get-tuple-element.7) | copy-start | bytes 1572868

commit v9 on v8

--- a/solution.py
+++ b/solution.py
@@ -34,7 +34,7 @@
     )
 
 
-def plane_steps(buf, full_sem, half_sem, send_sem):
+def plane_steps(buf, full_sem, half_sem, send_sem, upward=False):
     role, seq, tp = lax.axis_index("role"), lax.axis_index("seq"), lax.axis_index("tp")
     step_a, step_b = 1 + 3 * role, 4 - 3 * role
     z, x = seq // SIDE, seq % SIDE
@@ -53,14 +53,24 @@
         remote(
             buf.at[slot], buf.at[slot], send_sem.at[len(sent)], full_sem.at[slot], to_role, to_seq, tp
         ).start()
-        sent.append(2 * half)
+        sent.append((2 * half, False))
+
+    def mate(slot):
+        copy = remote(
+            buf.at[slot], buf.at[slot], send_sem.at[len(sent)], full_sem.at[slot], 1 - role, seq, tp
+        )
+        if upward:
+            pl.when(role == 0)(copy.start)
+        else:
+            copy.start()
+        sent.append((2 * half, upward))
 
     def part(slot, k, to_seq):
         piece = buf.at[slot, pl.ds(k * half, half)]
         remote(
             piece, piece, send_sem.at[len(sent)], half_sem.at[slot, k], role, to_seq, tp
         ).start()
-        sent.append(half)
+        sent.append((half, False))
 
     def wait_whole(slot):
         pltpu.make_async_copy(buf.at[slot], buf.at[slot], full_sem.at[slot]).wait()
@@ -73,18 +83,25 @@
     def spread_b(slot):
         whole(slot, role, seq_of(0, 1))
         whole(slot, role, seq_of(0, -1))
-        whole(slot, 1 - role, seq)
+        mate(slot)
 
     def pass_b(a):
         for b, k in ((-1, 0), (1, 1)):
             wait_whole(slot_of(a, b))
             part(slot_of(a, b), k, seq_of(0, -b))
-            whole(slot_of(a, b), 1 - role, seq)
+            mate(slot_of(a, b))
 
     def other(b):
         fixed = (ca + b + SIDE) % SIDE
-        for k in range(SIDE):
-            wait_whole((1 - role) * (SIDE * SIDE) + fixed * step_a + k * step_b)
+
+        def wait_all():
+            for k in range(SIDE):
+                wait_whole((1 - role) * (SIDE * SIDE) + fixed * step_a + k * step_b)
+
+        if upward:
+            pl.when(role == 1)(wait_all)
+        else:
+            wait_all()
 
     def start():
         own = slot_of(0, 0)
@@ -111,7 +128,7 @@
     def last():
         for a in (0, -1, 1, 2):
             wait_parts(slot_of(a, 2))
-            whole(slot_of(a, 2), 1 - role, seq)
+            mate(slot_of(a, 2))
         other(1)
 
     def mine(b):
@@ -134,9 +151,13 @@
     )
 
     def finish():
-        for n, rows in enumerate(sent):
+        for n, (rows, only_lower) in enumerate(sent):
             piece = buf.at[0, pl.ds(0, rows)]
-            pltpu.make_async_copy(piece, piece, send_sem.at[n]).wait()
+            done = pltpu.make_async_copy(piece, piece, send_sem.at[n])
+            if only_lower:
+                pl.when(role == 0)(done.wait)
+            else:
+                done.wait()
 
     return steps, finish
 
@@ -616,7 +637,7 @@
 
     keys[rank, :, :HEAD_DIM] = turned(heads)
     keys[rank, :, HEAD_DIM:] = sums[:, (heads + 1) * HEAD_DIM :].astype(jnp.bfloat16)
-    steps, k_sent = plane_steps(keys, k_full, k_half, k_send)
+    steps, k_sent = plane_steps(keys, k_full, k_half, k_send, upward=True)
     steps[0][0]()
     for h in range(heads):
         queries[h] = turned(h)

time: 136 us -> 136 us (level)
  no operation moved by 1% of the time
where the time goes in v9:
time: 136 us; the launch traced here: 135 us
  Pallas kernels  130 us (96%)
  local copies, waits for them, and re-layouts  3.16 us (2%)
    pallas_call x1, Pallas kernels, together(): pl.pallas_call(kernel, out_shape=(jax.ShapeDtypeStruct(prompt.shape, bf16...  130 us
    unnamed x4, local copies, waits for them, and re-layouts  3.16 us

profile of v9, /device:TPU:97, one launch (start us, length us, event | category | flops | bytes accessed | tf_op | source)
XLA Modules:
  0.0 135.2 jit_solution(15859289036325122306)
XLA Ops:
  0.7 1.2 multiply_sine_fusion
  1.9 130.2 %shard_map.95 = (bf16[256,2048]{1,0:T(8,128)(2,1)}, bf16[256,1024]{1,0:T(8,128)(2,1)}) custom-call(bf16[64,1280]{1,0:T(8,128)(2,1)} %hidden.1, bf16[1280,256]{1,0:T(8,128)(2,1)} %merger_out.1, s32[1,64]{1,0:T(1,128)} %bitcast.1, bf16[256,2048]{1,0:T(8,128)(2,1)} %prompt.1, bf16[2048]{0:T(1024)(128)(2,1)} %gain.1, bf16[8192,1024]{1,0:T(8,128)(2,1)} %query_weight.1, ...), custom_call_target="tpu_custom_call" | custom-call | tf_op jit(solution)/shard_map/pallas_call | solution.py:664
  132.1 0.0 copy-start
  132.1 2.4 %copy.12 = bf16[256,2048]{1,0:T(8,128)(2,1)} copy(bf16[256,2048]{1,0:T(8,128)(2,1)} %get-tuple-element.6) | data formatting | bytes 2097152
  134.4 0.0 copy-done
  134.4 0.8 copy.13
  (2 shorter events, 0.0 us)
Async XLA Ops:
  132.1 2.4 %copy-start = (bf16[256,1024]{1,0:T(8,128)(2,1)S(1)}, bf16[256,1024]{1,0:T(8,128)(2,1)}, u32[]{:S(2)}) copy-start(bf16[256,1024]{1,0:T(8,128)(2,1)} %get-tuple-element.7) | copy-start | bytes 1572868
